TPU v7x, 256 devices: a whole 4x4x8 slice. The times are simulated.
256 devices in a mesh: seq: 64 (over x, z, y_hi), tp: 4 (over y_lo, core).
Axes of the slice: x: 4, y: 4 (y_hi: 2, y_lo: 2; y = y_hi * 2 + y_lo), z: 8, core: 2. Of those that a mesh axis runs over, the one named last changes fastest.
Arguments:
- tree_hidden: bfloat16 [128, 8192], P(None, 'seq'), may hold values from -6 to 6
- query_low: bfloat16 [128, 8192], P('seq', 'tp'), may hold values from -24 to 24
- key_tree_low: bfloat16 [128, 1024], P('seq', 'tp'), may hold values from -20 to 20
- value_tree_low: bfloat16 [128, 1024], P('seq', 'tp'), may hold values from -6 to 6
- cache_keys: bfloat16 [8, 65536, 8, 128], P(None, 'seq', 'tp'), may hold values from -40 to 40
- cache_values: bfloat16 [8, 65536, 8, 128], P(None, 'seq', 'tp'), may hold values from -6 to 6
- cache_lengths: int32 [8], replicated, may hold values from 8192 to 65536
- ancestors: int32 [8, 16, 16], replicated, may hold values from 0 to 1, as said below
- out_weight: bfloat16 [8192, 8192], P('tp', 'seq'), may hold values from -0.0625 to 0.0625
- norm_gain: float32 [8192], P('seq'), may hold values from 0.1 to 1.9
- w_query_up: bfloat16 [8192, 8192], P('seq', 'tp'), may hold values from -0.0625 to 0.0625
- w_key_up: bfloat16 [8192, 1024], P('seq', 'tp'), may hold values from -0.5 to 0.5
- w_value_up: bfloat16 [8192, 1024], P('seq', 'tp'), may hold values from -0.0625 to 0.0625
- retained_keys: bfloat16 [64, 512, 8, 128], P('seq', None, 'tp'), may hold values from -400 to 400
- retained_values: bfloat16 [64, 512, 8, 128], P('seq', None, 'tp'), may hold values from -6 to 6
- retained_index: int32 [64, 512, 8], P('seq', None, 'tp'), may hold values from 0 to 65535
Outputs:
- residual: float32 [128, 8192], P(None, 'seq')
- upper_heads: float32 [128, 8192], P('seq', 'tp')
Inputs may be any that keep to these rules, and one draw needn't show every extreme that they name: ancestors[r, i, j] is 1 when node j is node i or an ancestor of node i in request r's tree, else 0; node 0 is the root and every other node's parent has a lower number.
All inputs are finite; a program needn't handle non-finite values.
Results may differ from a plain program's by a relative error of at most 0.04.
Values may be sent and summed in bfloat16 or wider, within the bound.
No kernel may reach another device: no remote copies, remote signals or barrier semaphores. Data moves between devices by JAX's collectives and lax.ppermute only.
A program may use at most 64 MiB of HBM per device.

v0:
```python
import math

import jax
import jax.numpy as jnp
from jax import lax
from jax.sharding import PartitionSpec as P

GROUP = 8


masked_score = -1e30
norm_epsilon = 1e-05


def in_one_piece(arrays, axis, dim, along):
    widths = [a.shape[along] for a in arrays]
    both = jnp.concatenate(arrays, axis=along)
    filled = lax.all_gather(both, axis, axis=dim, tiled=True)
    return tuple(jnp.split(filled, [sum(widths[:k]) for k in range(1, len(widths))], axis=along))


def side_by_side(arrays, axis, split_dim, concat_dim, along):
    widths = [math.prod(a.shape[along:]) for a in arrays]
    both = jnp.concatenate(
        [a.reshape(*a.shape[:along], w) for a, w in zip(arrays, widths)], axis=along
    )
    filled = lax.all_to_all(both, axis, split_axis=split_dim, concat_axis=concat_dim, tiled=True)
    blocks = jnp.split(filled, [sum(widths[:k]) for k in range(1, len(widths))], axis=along)
    return tuple(
        (b.reshape(*filled.shape[:along], *a.shape[along:]) for a, b in zip(arrays, blocks))
    )


def from_everyone(array, axis):
    copies = jnp.broadcast_to(array, (lax.axis_size(axis), *array.shape))
    return lax.all_to_all(copies, axis, split_axis=0, concat_axis=0, tiled=True)


def in_order(blocks, dim):
    blocks = jnp.moveaxis(blocks, 0, dim)
    lengths = blocks.shape
    return blocks.reshape(*lengths[:dim], lengths[dim] * lengths[dim + 1], *lengths[dim + 2 :])


def gather_directly(array, axis, dim):
    blocks = from_everyone(array, axis)
    return in_order(blocks, dim)


def of_everyone(array, axis):
    everything = from_everyone(array, axis)
    return jnp.sum(everything, axis=0)


def cut_along(array, dim, length):
    before, after = (array.shape[:dim], array.shape[dim + 1 :])
    return jnp.moveaxis(array.reshape(*before, length, -1, *after), dim, 0)


def sent_and_summed(array, axis, dim):
    blocks = cut_along(array, dim, lax.axis_size(axis))
    arrived = lax.all_to_all(blocks, axis, split_axis=0, concat_axis=0, tiled=True)
    return arrived.sum(axis=0)


def swapped(array, axis, apart):
    return lax.ppermute(array, axis, [(i, i ^ 1 << apart) for i in range(lax.axis_size(axis))])


def block_attend(query_rows, key_rows, value_rows, allowed_keys, kv_heads, head_dim):
    row_count = query_rows.shape[0]
    head_count = query_rows.shape[1] // head_dim
    group_size = head_count // kv_heads
    queries = query_rows.reshape(row_count, kv_heads, group_size, head_dim)
    scores = jnp.einsum(
        "nkgd,ckd->kgnc", queries, key_rows, preferred_element_type=jnp.float32
    ) * head_dim ** (-0.5)
    allowed = allowed_keys.T[:, None, None, :]
    masked = jnp.where(allowed, scores, masked_score)
    highest = jnp.max(masked, axis=-1)
    weights = jnp.where(allowed, jnp.exp(masked - highest[..., None]), 0.0)
    weight_sum = jnp.sum(weights, axis=-1)
    blended = jnp.einsum(
        "kgnc,ckd->nkgd",
        weights.astype(jnp.bfloat16),
        value_rows,
        preferred_element_type=jnp.float32,
    )
    return (
        blended.reshape(row_count, head_count, head_dim),
        highest.transpose(2, 0, 1).reshape(row_count, head_count),
        weight_sum.transpose(2, 0, 1).reshape(row_count, head_count),
    )


def tree_attend(query_rows, key_rows, value_rows, mask_rows, kv_heads, head_dim):
    row_count = query_rows.shape[0]
    head_count = query_rows.shape[1] // head_dim
    group_size = head_count // kv_heads
    queries = query_rows.reshape(row_count, kv_heads, group_size, head_dim)
    tree_keys = key_rows.reshape(-1, kv_heads, head_dim)
    tree_values = value_rows.reshape(-1, kv_heads, head_dim)
    scores = jnp.einsum(
        "nkgd,mkd->nkgm", queries, tree_keys, preferred_element_type=jnp.float32
    ) * head_dim ** (-0.5)
    allowed = (mask_rows > 0)[:, None, None, :]
    masked = jnp.where(allowed, scores, masked_score)
    highest = jnp.max(masked, axis=-1)
    weights = jnp.where(allowed, jnp.exp(masked - highest[..., None]), 0.0)
    weight_sum = jnp.sum(weights, axis=-1)
    blended = jnp.einsum(
        "nkgm,mkd->nkgd",
        weights.astype(jnp.bfloat16),
        tree_values,
        preferred_element_type=jnp.float32,
    )
    return (
        blended.reshape(row_count, head_count, head_dim),
        highest.reshape(row_count, head_count),
        weight_sum.reshape(row_count, head_count),
    )


def combine_parts(earlier, later):
    blend_early, high_early, sum_early = earlier
    blend_late, high_late, sum_late = later
    highest = jnp.maximum(high_early, high_late)
    factor_early = jnp.exp(high_early - highest)
    factor_late = jnp.exp(high_late - highest)
    return (
        blend_early * factor_early[..., None] + blend_late * factor_late[..., None],
        highest,
        sum_early * factor_early + sum_late * factor_late,
    )


def finish(partial_value, out_type):
    blended, highest, weight_sum = partial_value
    return (blended / weight_sum[..., None]).reshape(blended.shape[0], -1).astype(out_type)


def ordered_pair(mine, partner, upper_half):
    return jnp.where(
        upper_half,
        jnp.concatenate([partner, mine], axis=0),
        jnp.concatenate([mine, partner], axis=0),
    )


def shards(
    tree_hidden,
    query_low,
    key_tree_low,
    value_tree_low,
    cache_keys,
    cache_values,
    cache_lengths,
    ancestors,
    out_weight,
    norm_gain,
    w_query_up,
    w_key_up,
    w_value_up,
    retained_keys,
    retained_values,
    retained_index,
):
    seq_count = lax.axis_size("seq")
    seq_index = lax.axis_index("seq")
    requests, cache_part, kv_heads, head_dim = cache_keys.shape
    node_count = ancestors.shape[1]
    own_rows = query_low.shape[0]
    row_width = query_low.shape[1]
    all_rows = requests * node_count
    first_row = seq_index * own_rows
    request = first_row // node_count
    node_start = first_row % node_count
    tree_mask = lax.dynamic_slice_in_dim(
        lax.dynamic_index_in_dim(ancestors, request, 0, keepdims=False), node_start, own_rows, 0
    )
    seq_length = jnp.sum(
        jnp.where(jnp.arange(requests, dtype=jnp.int32) == request, cache_lengths, 0)
    )
    gathered_q, gathered_k, gathered_v = in_one_piece(
        (query_low, key_tree_low, value_tree_low), "seq", 0, 1
    )
    positions = seq_index * cache_part + jnp.arange(cache_part, dtype=jnp.int32)

    def cache_request(operands):
        query_rows, key_rows, value_rows, length_here = operands
        usable = jnp.broadcast_to((positions < length_here)[:, None], (cache_part, kv_heads))
        return block_attend(query_rows, key_rows, value_rows, usable, kv_heads, head_dim)

    part_blend, part_high, part_sum = lax.map(
        cache_request,
        (
            gathered_q.reshape(requests, node_count, row_width),
            cache_keys,
            cache_values,
            cache_lengths,
        ),
    )
    part_blend = part_blend.reshape(all_rows, -1, head_dim)
    part_high = part_high.reshape(all_rows, -1)
    part_sum = part_sum.reshape(all_rows, -1)
    spread_blend, spread_high, spread_sum = side_by_side(
        (part_blend[None], part_high[None], part_sum[None]), "seq", 1, 0, 3
    )
    highest = jnp.max(spread_high, axis=0)
    factor = jnp.exp(spread_high - highest[None])
    cache_merged = (
        jnp.sum(spread_blend * factor[..., None], axis=0),
        highest,
        jnp.sum(spread_sum * factor, axis=0),
    )
    request_keys = lax.dynamic_slice_in_dim(gathered_k, request * node_count, node_count, 0)
    request_values = lax.dynamic_slice_in_dim(gathered_v, request * node_count, node_count, 0)
    own_heads = finish(
        combine_parts(
            cache_merged,
            tree_attend(query_low, request_keys, request_values, tree_mask, kv_heads, head_dim),
        ),
        jnp.bfloat16,
    )
    lower_all = gather_directly(own_heads, "seq", 0)
    head_terms = jnp.dot(lower_all, out_weight, preferred_element_type=jnp.float32)
    summed = of_everyone(head_terms, "tp")
    residual = tree_hidden.astype(jnp.float32) + summed
    squares = of_everyone(jnp.sum(residual * residual, axis=1), "seq")
    model_width = residual.shape[1] * seq_count
    inverse = lax.rsqrt(squares / model_width + norm_epsilon)
    normed = (residual * inverse[:, None] * norm_gain[None, :]).astype(jnp.bfloat16)
    projected = sent_and_summed(
        jnp.concatenate(
            [
                jnp.dot(normed, w_query_up, preferred_element_type=jnp.float32),
                jnp.dot(normed, w_key_up, preferred_element_type=jnp.float32),
                jnp.dot(normed, w_value_up, preferred_element_type=jnp.float32),
            ],
            axis=1,
        ),
        "seq",
        0,
    )
    kv_width = w_key_up.shape[1]
    query_up = projected[:, :row_width].astype(jnp.bfloat16)
    key_up = projected[:, row_width : row_width + kv_width].astype(jnp.bfloat16)
    value_up = projected[:, row_width + kv_width :].astype(jnp.bfloat16)
    levels = GROUP.bit_length() - 1
    keys_here = retained_keys[0]
    values_here = retained_values[0]
    index_here = retained_index[0]
    rows_query, rows_key, rows_value = (query_up, key_up, value_up)
    for level in range(levels):
        other_query, other_key, other_value = swapped(
            (rows_query, rows_key, rows_value), "seq", level
        )
        upper_half = jnp.right_shift(seq_index, level) % 2 == 1
        rows_query = ordered_pair(rows_query, other_query, upper_half)
        rows_key = ordered_pair(rows_key, other_key, upper_half)
        rows_value = ordered_pair(rows_value, other_value, upper_half)
    partial_value = block_attend(
        rows_query, keys_here, values_here, index_here < seq_length, kv_heads, head_dim
    )
    for level in range(levels):
        partner = swapped((partial_value[0], partial_value[1], partial_value[2]), "seq", level)
        partial_value = combine_parts(partial_value, partner)
    own_parts = (
        lax.dynamic_slice_in_dim(partial_value[0], node_start, own_rows, 0),
        lax.dynamic_slice_in_dim(partial_value[1], node_start, own_rows, 0),
        lax.dynamic_slice_in_dim(partial_value[2], node_start, own_rows, 0),
    )
    upper_heads = finish(
        combine_parts(
            own_parts, tree_attend(query_up, rows_key, rows_value, tree_mask, kv_heads, head_dim)
        ),
        jnp.float32,
    )
    return (residual, upper_heads)


def solution(mesh):
    return jax.shard_map(
        shards,
        mesh=mesh,
        in_specs=(
            P(None, "seq"),
            P("seq", "tp"),
            P("seq", "tp"),
            P("seq", "tp"),
            P(None, "seq", "tp", None),
            P(None, "seq", "tp", None),
            P(),
            P(),
            P("tp", "seq"),
            P("seq"),
            P("seq", "tp"),
            P("seq", "tp"),
            P("seq", "tp"),
            P("seq", None, "tp", None),
            P("seq", None, "tp", None),
            P("seq", None, "tp"),
        ),
        out_specs=(P(None, "seq"), P("seq", "tp")),
        check_vma=False,
    )
```

profile of v0, /device:TPU:8, one launch (start us, length us, event | category | flops | bytes accessed | tf_op | source)
XLA Modules:
  0.0 441.0 jit_solution(17505832320885540647)
XLA Ops:
  1.5 187.3 %all-gather = bf16[64,2,2560]{2,1,0:T(2,128)(2,1)S(1)} all-gather(bf16[1,2,2560]{2,1,0:T(2,128)(2,1)S(1)} %maximum_bitcast_fusion.1), channel_id=1, replica_groups=mesh['seq'=64,'tp'=4] {'seq'}, dimensions={0}, use_global_device_ids=true | all-gather | bytes 665600 | tf_op jit(solution)/shard_map/all_gather | solution.py:18
  189.1 48.1 %while.15 = (s32[]{:T(128)}, f32[8,16,16,128]{3,2,1,0:T(8,128)}, f32[8,16,16]{2,1,0:T(8,128)S(1)}, f32[8,16,16]{2,1,0:T(8,128)S(1)}, bf16[8,1024,2,128]{3,2,1,0:...) while((s32[]{:T(128)}, f32[8,16,16,128]{3,2,1,0:T(8,128)}, ...), condition=%wide.region_3.4_spmd.clone, body=%wide.region_0.3_spmd.clone.sunk | while | flops 136578560 | bytes 7057557 | solution.py:194
  238.4 3.0 maximum_bitcast_fusion
  241.4 4.8 %all-to-all-start = ((f32[1,128,16,130]{3,2,0,1:T(8,128)}), f32[1,128,16,130]{3,2,0,1:T(8,128)S(1)}, u32[]{:S(2)}, u32[]{:S(2)}) async-start(f32[1,128,16,130]{3,2,0,1:T(8,128)} %maximum_bitcast_fusion), calls=%async_computation | async-start | bytes 4194304 | tf_op jit(solution)/shard_map/all_to_all | solution.py:27
  247.8 36.0 %all-to-all-done = f32[1,128,16,130]{3,2,0,1:T(8,128)S(1)} async-done(((f32[1,128,16,130]{3,2,0,1:T(8,128)}), f32[1,128,16,130]{3,2,0,1:T(8,128)S(1)}, u32[]{:S(2)}, u32[]{:S(2)}) %all-to-all-start) | async-done | bytes 1064992 | tf_op jit(solution)/shard_map/all_to_all | solution.py:27
  285.4 1.8 copy.425
  287.2 1.8 copy.485
  290.2 20.7 %all_to_all.33 = bf16[64,2,2048]{2,1,0:T(2,128)(2,1)S(1)} all-to-all(bf16[64,2,2048]{2,1,0:T(2,128)(2,1)S(1)} %broadcast_in_dim.125), channel_id=1, replica_groups=mesh['seq'=64,'tp'=4] {'seq'}, dimensions={0} | all-to-all | bytes 1048576 | tf_op jit(solution)/shard_map/all_to_all | solution.py:36
  312.5 8.2 %all_to_all.34 = f32[4,128,128]{2,1,0:T(8,128)S(1)} all-to-all(f32[4,128,128]{2,1,0:T(8,128)S(1)} %broadcast_in_dim.126), channel_id=1, replica_groups=mesh['seq'=64,'tp'=4] {'tp'}, dimensions={0} | all-to-all | bytes 524288 | tf_op jit(solution)/shard_map/all_to_all | solution.py:36
  320.9 17.2 %all_to_all.35 = f32[64,1,128]{2,1,0:T(1,128)S(1)} all-to-all(f32[64,1,128]{2,1,0:T(1,128)S(1)} %broadcast_in_dim.130), channel_id=1, replica_groups=mesh['seq'=64,'tp'=4] {'seq'}, dimensions={0} | all-to-all | bytes 65536 | tf_op jit(solution)/shard_map/all_to_all | solution.py:36
  338.9 1.8 reshape.201
  340.8 5.0 %all-to-all-start.4 = ((f32[64,2,2560]{2,1,0:T(2,128)}), f32[64,2,2560]{2,1,0:T(2,128)S(1)}, u32[]{:S(2)}, u32[]{:S(2)}) async-start(f32[64,2,2560]{2,1,0:T(2,128)} %reshape.201), calls=%async_computation.4 | async-start | bytes 2621440 | tf_op jit(solution)/shard_map/all_to_all | solution.py:62
  347.1 33.4 %all-to-all-done.4 = f32[64,2,2560]{2,1,0:T(2,128)S(1)} async-done(((f32[64,2,2560]{2,1,0:T(2,128)}), f32[64,2,2560]{2,1,0:T(2,128)S(1)}, u32[]{:S(2)}, u32[]{:S(2)}) %all-to-all-start.4) | async-done | bytes 1310752 | tf_op jit(solution)/shard_map/all_to_all | solution.py:62
  381.5 3.2 collective-permute-start.12
  388.4 2.0 collective-permute-done.13
  393.5 3.0 collective-permute-done.11
  398.4 2.2 collective-permute-done.1
  402.3 3.2 collective-permute-done.2
  406.4 1.7 collective-permute-start.3
  408.1 1.8 collective-permute-start.15
  418.0 2.8 collective-permute-start.7
  423.9 3.8 collective-permute-done.4
  429.3 3.6 collective-permute-done.6
  433.3 7.0 %collective-permute-done.8 = f32[16,16,128]{2,1,0:T(8,128)S(1)} collective-permute-done((f32[16,16,128]{2,1,0:T(8,128)S(1)}, f32[16,16,128]{2,1,0:T(8,128)S(1)}, u32[]{:S(2)}, u32[]{:S(2)}) %collective-permute-start.8) | collective-permute-done | bytes 131104 | tf_op jit(solution)/shard_map/ppermute | solution.py:67
  (241 shorter events, 84.2 us)
Async XLA Ops:
  0.6 337.9 %copy-start = (bf16[128,2048]{1,0:T(8,128)(2,1)S(1)}, bf16[128,2048]{1,0:T(8,128)(2,1)}, u32[]{:S(2)}) copy-start(bf16[128,2048]{1,0:T(8,128)(2,1)} %param.28) | copy-start | bytes 1572868
  0.6 188.4 %copy-start.10 = (s32[8]{0:T(128)S(1)}, s32[8]{0:T(128)}, u32[]{:S(2)}) copy-start(s32[8]{0:T(128)} %param.24) | copy-start | bytes 100
  241.4 42.4 %all-to-all-start = ((f32[1,128,16,130]{3,2,0,1:T(8,128)}), f32[1,128,16,130]{3,2,0,1:T(8,128)S(1)}, u32[]{:S(2)}, u32[]{:S(2)}) async-start(f32[1,128,16,130]{3,2,0,1:T(8,128)} %maximum_bitcast_fusion), calls=%async_computation | async-start | bytes 4194304 | tf_op jit(solution)/shard_map/all_to_all | solution.py:27
  340.8 64.7 %copy-start.8 = (bf16[1,512,2,128]{3,2,1,0:T(2,128)(2,1)S(1)}, bf16[1,512,2,128]{3,2,1,0:T(2,128)(2,1)}, u32[]{:S(2)}) copy-start(bf16[1,512,2,128]{3,2,1,0:T(2,128)(2,1)} %param.31) | copy-start | bytes 786436
  340.8 39.7 %all-to-all-start.4 = ((f32[64,2,2560]{2,1,0:T(2,128)}), f32[64,2,2560]{2,1,0:T(2,128)S(1)}, u32[]{:S(2)}, u32[]{:S(2)}) async-start(f32[64,2,2560]{2,1,0:T(2,128)} %reshape.201), calls=%async_computation.4 | async-start | bytes 2621440 | tf_op jit(solution)/shard_map/all_to_all | solution.py:62
  345.8 75.0 %copy-start.9 = (bf16[1,512,2,128]{3,2,1,0:T(2,128)(2,1)S(1)}, bf16[1,512,2,128]{3,2,1,0:T(2,128)(2,1)}, u32[]{:S(2)}) copy-start(bf16[1,512,2,128]{3,2,1,0:T(2,128)(2,1)} %param.32) | copy-start | bytes 786436
  381.0 5.2 %collective-permute-start.9 = (bf16[2,256]{1,0:T(2,128)(2,1)S(1)}, bf16[2,256]{1,0:T(2,128)(2,1)S(1)}, u32[]{:S(2)}, u32[]{:S(2)}) collective-permute-start(bf16[2,256]{1,0:T(2,128)(2,1)S(1)} %get-tuple-element.208), channel_id=1, source_target_pairs={{0,4},{4,0},{8,12},{12,8},{16,20},{20,16},{24,28},{28,24},{32,36},... | collective-permute-start | bytes 3080 | tf_op jit(solution)/shard_map/ppermute | solution.py:67
  381.5 5.2 %collective-permute-start.12 = (bf16[2,256]{1,0:T(2,128)(2,1)S(1)}, bf16[2,256]{1,0:T(2,128)(2,1)S(1)}, u32[]{:S(2)}, u32[]{:S(2)}) collective-permute-start(bf16[2,256]{1,0:T(2,128)(2,1)S(1)} %get-tuple-element.205), channel_id=1, source_target_pairs={{0,4},{4,0},{8,12},{12,8},{16,20},{20,16},{24,28},{28,24},{32,36},... | collective-permute-start | bytes 3080 | tf_op jit(solution)/shard_map/ppermute | solution.py:67
  384.7 12.0 %collective-permute-start = (bf16[2,2048]{1,0:T(2,128)(2,1)S(1)}, bf16[2,2048]{1,0:T(2,128)(2,1)S(1)}, u32[]{:S(2)}, u32[]{:S(2)}) collective-permute-start(bf16[2,2048]{1,0:T(2,128)(2,1)S(1)} %get-tuple-element.209), channel_id=1, source_target_pairs={{0,4},{4,0},{8,12},{12,8},{16,20},{20,16},{24,28},{28,24},{32,36},... | collective-permute-start | bytes 24584 | tf_op jit(solution)/shard_map/ppermute | solution.py:67
  386.1 5.7 %collective-permute-start.10 = (bf16[4,256]{1,0:T(4,128)(2,1)S(1)}, bf16[4,256]{1,0:T(4,128)(2,1)S(1)}, u32[]{:S(2)}, u32[]{:S(2)}) collective-permute-start(bf16[4,256]{1,0:T(4,128)(2,1)S(1)} %maximum_select_fusion.11), channel_id=1, source_target_pairs={{0,8},{4,12},{8,0},{12,4},{16,24},{20,28},{24,16},{28,20},{32,40},... | collective-permute-start | bytes 6152 | tf_op jit(solution)/shard_map/ppermute | solution.py:67
  386.7 3.7 collective-permute-start.13
  390.4 19.6 %collective-permute-start.14 = (bf16[8,256]{1,0:T(8,128)(2,1)S(1)}, bf16[8,256]{1,0:T(8,128)(2,1)S(1)}, u32[]{:S(2)}, u32[]{:S(2)}) collective-permute-start(bf16[8,256]{1,0:T(8,128)(2,1)S(1)} %maximum_select_fusion.9), channel_id=1, source_target_pairs={{0,16},{4,20},{8,24},{12,28},{16,0},{20,4},{24,8},{28,12},{32,48},... | collective-permute-start | bytes 12296 | tf_op jit(solution)/shard_map/ppermute | solution.py:67
  391.9 4.6 %collective-permute-start.11 = (bf16[8,256]{1,0:T(8,128)(2,1)S(1)}, bf16[8,256]{1,0:T(8,128)(2,1)S(1)}, u32[]{:S(2)}, u32[]{:S(2)}) collective-permute-start(bf16[8,256]{1,0:T(8,128)(2,1)S(1)} %maximum_select_fusion.7), channel_id=1, source_target_pairs={{0,16},{4,20},{8,24},{12,28},{16,0},{20,4},{24,8},{28,12},{32,48},... | collective-permute-start | bytes 12296 | tf_op jit(solution)/shard_map/ppermute | solution.py:67
  396.7 3.8 collective-permute-start.1
  400.6 4.9 %collective-permute-start.2 = (bf16[8,2048]{1,0:T(8,128)(2,1)S(1)}, bf16[8,2048]{1,0:T(8,128)(2,1)S(1)}, u32[]{:S(2)}, u32[]{:S(2)}) collective-permute-start(bf16[8,2048]{1,0:T(8,128)(2,1)S(1)} %maximum_select_fusion.1), channel_id=1, source_target_pairs={{0,16},{4,20},{8,24},{12,28},{16,0},{20,4},{24,8},{28,12},{32,48},... | collective-permute-start | bytes 98312 | tf_op jit(solution)/shard_map/ppermute | solution.py:67
  406.4 5.2 %collective-permute-start.3 = (f32[16,16]{1,0:T(8,128)S(1)}, f32[16,16]{1,0:T(8,128)S(1)}, u32[]{:S(2)}, u32[]{:S(2)}) collective-permute-start(f32[16,16]{1,0:T(8,128)S(1)} %copy.435), channel_id=1, source_target_pairs={{0,4},{4,0},{8,12},{12,8},{16,20},{20,16},{24,28},{28,24},{32,36},... | collective-permute-start | bytes 3080 | tf_op jit(solution)/shard_map/ppermute | solution.py:67
  408.1 5.2 %collective-permute-start.15 = (f32[16,16]{1,0:T(8,128)S(1)}, f32[16,16]{1,0:T(8,128)S(1)}, u32[]{:S(2)}, u32[]{:S(2)}) collective-permute-start(f32[16,16]{1,0:T(8,128)S(1)} %copy.454), channel_id=1, source_target_pairs={{0,4},{4,0},{8,12},{12,8},{16,20},{20,16},{24,28},{28,24},{32,36},... | collective-permute-start | bytes 3080 | tf_op jit(solution)/shard_map/ppermute | solution.py:67
  413.3 3.7 collective-permute-start.16
  414.3 3.7 collective-permute-start.5
  418.0 5.9 %collective-permute-start.7 = (f32[16,16]{1,0:T(8,128)S(1)}, f32[16,16]{1,0:T(8,128)S(1)}, u32[]{:S(2)}, u32[]{:S(2)}) collective-permute-start(f32[16,16]{1,0:T(8,128)S(1)} %get-tuple-element.182), channel_id=1, source_target_pairs={{0,16},{4,20},{8,24},{12,28},{16,0},{20,4},{24,8},{28,12},{32,48},... | collective-permute-start | bytes 3080 | tf_op jit(solution)/shard_map/ppermute | solution.py:67
  421.1 6.6 %collective-permute-start.4 = (f32[16,16,128]{2,1,0:T(8,128)S(1)}, f32[16,16,128]{2,1,0:T(8,128)S(1)}, u32[]{:S(2)}, u32[]{:S(2)}) collective-permute-start(f32[16,16,128]{2,1,0:T(8,128)S(1)} %copy.436), channel_id=1, source_target_pairs={{0,4},{4,0},{8,12},{12,8},{16,20},{20,16},{24,28},{28,24},{32,36},... | collective-permute-start | bytes 393224 | tf_op jit(solution)/shard_map/ppermute | solution.py:67
  422.8 10.5 %collective-permute-start.17 = (f32[16,16]{1,0:T(8,128)S(1)}, f32[16,16]{1,0:T(8,128)S(1)}, u32[]{:S(2)}, u32[]{:S(2)}) collective-permute-start(f32[16,16]{1,0:T(8,128)S(1)} %get-tuple-element.179), channel_id=1, source_target_pairs={{0,16},{4,20},{8,24},{12,28},{16,0},{20,4},{24,8},{28,12},{32,48},... | collective-permute-start | bytes 3080 | tf_op jit(solution)/shard_map/ppermute | solution.py:67
  427.8 5.1 %collective-permute-start.6 = (f32[16,16,128]{2,1,0:T(8,128)S(1)}, f32[16,16,128]{2,1,0:T(8,128)S(1)}, u32[]{:S(2)}, u32[]{:S(2)}) collective-permute-start(f32[16,16,128]{2,1,0:T(8,128)S(1)} %multiply_add_fusion.1), channel_id=1, source_target_pairs={{0,8},{4,12},{8,0},{12,4},{16,24},{20,28},{24,16},{28,20},{32,40},... | collective-permute-start | bytes 393224 | tf_op jit(solution)/shard_map/ppermute | solution.py:67
  433.0 7.4 %collective-permute-start.8 = (f32[16,16,128]{2,1,0:T(8,128)S(1)}, f32[16,16,128]{2,1,0:T(8,128)S(1)}, u32[]{:S(2)}, u32[]{:S(2)}) collective-permute-start(f32[16,16,128]{2,1,0:T(8,128)S(1)} %multiply_add_fusion), channel_id=1, source_target_pairs={{0,16},{4,20},{8,24},{12,28},{16,0},{20,4},{24,8},{28,12},{32,48},... | collective-permute-start | bytes 393224 | tf_op jit(solution)/shard_map/ppermute | solution.py:67
  (7 other events, 164.4 us)
where the time goes:
time: 444 us; the launch traced here: 441 us
  blocking collectives  233 us (52%)
  waiting for transfers between devices  101 us (23%)
  local copies, waits for them, and re-layouts  43.5 us (10%)
  starting transfers between devices  35.3 us (8%)
  other arithmetic  17.4 us (4%)
  matrix products  9.15 us (2%)
    all_gather x1, blocking collectives, in_one_piece(): filled = lax.all_gather(both, axis, axis=dim, tiled=True)  187 us
    all_to_all x3, blocking collectives, from_everyone(): return lax.all_to_all(copies, axis, split_axis=0, concat_axis=0, tiled=True)  46.1 us
    all_to_all x1, waiting for transfers between devices, side_by_side(): lax.all_to_all(both, axis, split_axis=split_dim, concat_axis=concat_dim,...  36 us
    all_to_all x1, waiting for transfers between devices, sent_and_summed(): lax.all_to_all(blocks, axis, split_axis=0, concat_axis=0, tiled=True)  33.4 us
    ppermute x18, waiting for transfers between devices, swapped(): lax.ppermute(array, axis, [(i, i ^ 1 << apart) for i in range(lax.axis_si...  31.4 us
    dynamic_slice x24, local copies, waits for them, and re-layouts, shards(): lax.map(cache_request, (gathered_q.reshape(requests, node_count, row_widt...  27.5 us
    ppermute x18, starting transfers between devices, swapped(): lax.ppermute(array, axis, [(i, i ^ 1 << apart) for i in range(lax.axis_si...  25.5 us
  transfers between devices with their start and end apart: 20, of which 15 were waited for; matrix products, arithmetic and copies ran while one was open for 1% of the time, Pallas kernels for 0%

commit v1 on v0

v1 whole, which is shorter than its diff:
```python
import functools

import jax
import jax.numpy as jnp
from jax import lax
from jax.experimental import pallas as pl
from jax.experimental.pallas import tpu as pltpu
from jax.sharding import Mesh, PartitionSpec as P

HD = 128
GROUP = 8
SCALE = HD ** (-0.5)
SCALE2 = SCALE * 1.4426950408889634
MASKED = -1e30
FLOOR = -1e20
EPS = 1e-05
F32 = jnp.float32
BF16 = jnp.bfloat16

SEQ = ("x", "zh", "zl", "yh")
TEAM = ("zl", "yh")


def contract(a, b, dims):
    return lax.dot_general(a, b, (dims, ((), ())), preferred_element_type=F32)


def exchanged(blocks, axis):
    return lax.all_to_all(blocks, axis, split_axis=0, concat_axis=0, tiled=True)


def spread(array, axis):
    copies = jnp.broadcast_to(array, (lax.axis_size(axis), *array.shape))
    return exchanged(copies, axis)


def head_halves(rows):
    parity = lax.broadcasted_iota(jnp.int32, (16, HD), 0) % 2
    even = (parity == 0).astype(F32).astype(BF16)
    odd = (parity == 1).astype(F32).astype(BF16)
    count = rows.shape[0] // 16
    tiles = rows.reshape(count, 16, HD)
    first = (tiles * even[None]).reshape(rows.shape)
    second = (tiles * odd[None]).reshape(rows.shape)
    return jnp.concatenate([first, second], axis=1)


def pair_max(scores):
    width = scores.shape[1]
    folded = scores[:, 0:HD]
    for c in range(HD, width, HD):
        folded = jnp.maximum(folded, scores[:, c : c + HD])
    odd = lax.broadcasted_iota(jnp.int32, folded.shape, 1) % 2 == 1
    m0 = jnp.max(jnp.where(odd, MASKED, folded), axis=1, keepdims=True)
    m1 = jnp.max(jnp.where(odd, folded, MASKED), axis=1, keepdims=True)
    return m0, m1, odd


def shift_of(maximum):
    return jnp.maximum(maximum, FLOOR).astype(BF16).astype(F32)


def pair_weights(scores, s0, s1, odd):
    width = scores.shape[1]
    shift = jnp.where(odd, s1, s0)
    pieces = []
    total = jnp.zeros((scores.shape[0], HD), F32)
    for c in range(0, width, HD):
        w = jnp.exp2(scores[:, c : c + HD] - shift)
        total = total + w
        pieces.append(w.astype(BF16))
    l0 = jnp.sum(jnp.where(odd, 0.0, total), axis=1, keepdims=True)
    l1 = jnp.sum(jnp.where(odd, total, 0.0), axis=1, keepdims=True)
    return jnp.concatenate(pieces, axis=1), l0, l1


def stat_tile(s0, s1, l0, l1):
    lane = lax.broadcasted_iota(jnp.int32, (s0.shape[0], HD), 1)
    return jnp.where(
        lane < 64, jnp.where(lane < 32, s0, s1), jnp.where(lane < 96, l0, l1)
    )


def turn_kernel(k_hbm, kt_ref, k_buf, sems):
    requests, keys, _ = k_buf.shape
    step = 256

    def copy(r):
        return pltpu.make_async_copy(k_hbm.at[r], k_buf.at[r], sems.at[r])

    for r in range(requests):
        copy(r).start()
    for r in range(requests):
        copy(r).wait()
        for c in range(0, keys, step):
            kt_ref[r, :, c : c + step] = k_buf[r, c : c + step, :].T


def turn(keys):
    requests, count, _ = keys.shape
    return pl.pallas_call(
        turn_kernel,
        in_specs=[pl.BlockSpec(memory_space=pltpu.HBM)],
        out_specs=pl.BlockSpec(memory_space=pltpu.VMEM),
        out_shape=jax.ShapeDtypeStruct((requests, HD, count), BF16),
        scratch_shapes=[
            pltpu.VMEM((requests, count, HD), BF16),
            pltpu.SemaphoreType.DMA((requests,)),
        ],
        compiler_params=pltpu.CompilerParams(vmem_limit_bytes=8 << 20),
        name="turn",
    )(pltpu.with_memory_space_constraint(keys, pltpu.HBM))


def cache_kernel(
    len_ref, q_ref, kt_hbm, v_hbm, kv_ref, out_ref, first_scr, second_scr, k_buf, v_buf, sems
):
    requests, _, keys = k_buf.shape

    def fetch_keys(r):
        return pltpu.make_async_copy(kt_hbm.at[r], k_buf.at[r], sems.at[0, r])

    def fetch_values(r):
        return pltpu.make_async_copy(v_hbm.at[r], v_buf.at[r], sems.at[1, r])

    for r in range(requests):
        fetch_keys(r).start()
        fetch_values(r).start()
    start = lax.axis_index(SEQ) * (keys // 2)
    rows = 16 * GROUP
    step = 256
    kv_own = kv_ref[...].astype(F32)
    odd = lax.broadcasted_iota(jnp.int32, (rows, HD), 1) % 2 == 1
    lane = lax.broadcasted_iota(jnp.int32, (8, HD), 1)
    column = lax.broadcasted_iota(jnp.int32, (1, step), 1)
    first_head = (column % 2 == 0).astype(F32).astype(BF16)
    second_head = (column % 2 == 1).astype(F32).astype(BF16)

    def score(r, scr):
        block = q_ref[r * GROUP : (r + 1) * GROUP]
        queries = jnp.concatenate(
            [block[:, 0:16, :].reshape(rows, HD), block[:, 16:32, :].reshape(rows, HD)], axis=1
        )
        limit = 2 * (len_ref[r] - start)
        folded = None
        for c in range(0, keys, step):
            turned = k_buf[r, :, c : c + step]
            both = jnp.concatenate([turned * first_head, turned * second_head], axis=0)
            part = contract(queries, both, ((1,), (0,))) * SCALE2
            part = part + jnp.where(column + c < limit, 0.0, MASKED)
            scr[:, c : c + step] = part
            for d in range(0, step, HD):
                piece = part[:, d : d + HD]
                folded = piece if folded is None else jnp.maximum(folded, piece)
        return folded

    def blend(r, scr, folded):
        s0 = shift_of(jnp.max(jnp.where(odd, MASKED, folded), axis=1, keepdims=True))
        s1 = shift_of(jnp.max(jnp.where(odd, folded, MASKED), axis=1, keepdims=True))
        shift = jnp.where(odd, s1, s0)
        total = jnp.zeros((rows, HD), F32)
        mixed = jnp.zeros((rows, 2 * HD), F32)
        for c in range(0, keys, step):
            pieces = []
            for d in range(c, c + step, HD):
                w = jnp.exp2(scr[:, d : d + HD] - shift)
                total = total + w
                pieces.append(w.astype(BF16))
            mixed = mixed + contract(
                jnp.concatenate(pieces, axis=1),
                head_halves(v_buf[r, c : c + step, :]),
                ((1,), (0,)),
            )
        l0 = jnp.sum(jnp.where(odd, 0.0, total), axis=1, keepdims=True)
        l1 = jnp.sum(jnp.where(odd, total, 0.0), axis=1, keepdims=True)
        stats = stat_tile(s0, s1, l0, l1)
        for j in range(GROUP):
            low, high, at = 16 * j, 16 * j + 16, r * GROUP + j
            out_ref[at, 0:16, :] = mixed[low:high, 0:HD].astype(BF16)
            out_ref[at, 16:32, :] = mixed[low:high, HD:].astype(BF16)
            pair = jnp.where(lane % 2 == 0, stats[low : low + 8], stats[low + 8 : high])
            out_ref[at, 32:48, :] = jnp.concatenate([pair, kv_own], axis=0).astype(BF16)

    scratch = (first_scr, second_scr)
    fetch_keys(0).wait()
    folded = score(0, scratch[0])
    for r in range(requests):
        if r + 1 < requests:
            fetch_keys(r + 1).wait()
        fetch_values(r).wait()
        ahead = score(r + 1, scratch[(r + 1) % 2]) if r + 1 < requests else None
        blend(r, scratch[r % 2], folded)
        folded = ahead


def cache_attend(lengths, queries, keys, values, kv_own):
    requests, _, count = keys.shape
    vmem = pl.BlockSpec(memory_space=pltpu.VMEM)
    return pl.pallas_call(
        cache_kernel,
        in_specs=[
            pl.BlockSpec(memory_space=pltpu.SMEM),
            vmem,
            pl.BlockSpec(memory_space=pltpu.HBM),
            pl.BlockSpec(memory_space=pltpu.HBM),
            vmem,
        ],
        out_specs=vmem,
        out_shape=jax.ShapeDtypeStruct((requests * GROUP, 48, HD), BF16),
        scratch_shapes=[
            pltpu.VMEM((16 * GROUP, count), F32),
            pltpu.VMEM((16 * GROUP, count), F32),
            pltpu.VMEM((requests, HD, count), BF16),
            pltpu.VMEM((requests, count, HD), BF16),
            pltpu.SemaphoreType.DMA((2, requests)),
        ],
        compiler_params=pltpu.CompilerParams(vmem_limit_bytes=20 << 20),
        name="cache_attend",
    )(
        lengths,
        queries,
        pltpu.with_memory_space_constraint(keys, pltpu.HBM),
        pltpu.with_memory_space_constraint(values, pltpu.HBM),
        kv_own,
    )


def merge_kernel(parts_ref, q_ref, anc_ref, out_ref):
    place = lax.axis_index(SEQ)
    request = place // GROUP
    node = 2 * (place % GROUP)
    first = pl.multiple_of(request * GROUP, GROUP)
    tree = parts_ref[pl.ds(first, GROUP), 32:48, :].astype(F32)[:, 8:16, :].reshape(64, HD)
    tree_values = pltpu.roll(tree, 60, 0)
    tree_keys = tree.astype(BF16)
    row = lax.broadcasted_iota(jnp.int32, (32, 64), 0)
    col = lax.broadcasted_iota(jnp.int32, (32, 64), 1)
    picks = (
        lax.broadcasted_iota(jnp.int32, (16, 64), 0)
        == 2 * (lax.broadcasted_iota(jnp.int32, (16, 64), 1) // 8)
        + lax.broadcasted_iota(jnp.int32, (16, 64), 1) % 2
    )
    ancestry = contract(
        anc_ref[request].astype(F32).astype(BF16), picks.astype(F32).astype(BF16), ((1,), (0,))
    )
    which = lax.broadcasted_iota(jnp.int32, (16, 64), 0)
    mine0 = jnp.sum(jnp.where(which == node, ancestry, 0.0), axis=0, keepdims=True)
    mine1 = jnp.sum(jnp.where(which == node + 1, ancestry, 0.0), axis=0, keepdims=True)
    seen = jnp.where((row // 8) % 2 == 0, mine0, mine1)
    allowed = (seen > 0.5) & ((col // 4) % 2 == 0) & ((col // 2) % 2 == row // 16)
    scores = contract(q_ref[...], tree_keys, ((1,), (1,))) * SCALE2
    scores = jnp.where(allowed, scores, MASKED)
    m_tree = jnp.max(scores, axis=1, keepdims=True)
    w_tree = jnp.where(allowed, jnp.exp2(scores - m_tree), 0.0)
    l_tree = jnp.sum(w_tree, axis=1, keepdims=True)
    o_tree = contract(w_tree.astype(BF16), tree_values.astype(BF16), ((1,), (0,)))

    stats = parts_ref[:, 32:48, :].astype(F32)[:, 0:8, :]
    highest = jnp.max(stats, axis=0)
    factor = jnp.exp2(jnp.minimum(stats - highest[None], 0.0))
    sums = pltpu.roll(stats.reshape(-1, HD), 64, 1).reshape(stats.shape)
    total = jnp.sum(sums * factor, axis=0)
    for h in range(2):
        both = parts_ref[:, 16 * h : 16 * h + 16, :].astype(F32)
        for i in range(2):
            lane = h * 32 + i
            at = 16 * h + 8 * i
            blend = jnp.sum(both[:, 8 * i : 8 * i + 8, :] * factor[:, :, lane : lane + 1], axis=0)
            m_far = highest[:, lane : lane + 1]
            m_near = m_tree[at : at + 8]
            top = jnp.maximum(m_far, m_near)
            f_far = jnp.exp2(m_far - top)
            f_near = jnp.exp2(m_near - top)
            denominator = total[:, lane : lane + 1] * f_far + l_tree[at : at + 8] * f_near
            heads = (blend * f_far + o_tree[at : at + 8] * f_near) / denominator
            for g in range(8):
                out_ref[i : i + 1, (8 * h + g) * HD : (8 * h + g + 1) * HD] = heads[g : g + 1]


def merge_lower(parts, own_q, ancestors):
    return pl.pallas_call(
        merge_kernel,
        in_specs=[pl.BlockSpec(memory_space=pltpu.VMEM)] * 3,
        out_specs=pl.BlockSpec(memory_space=pltpu.VMEM),
        out_shape=jax.ShapeDtypeStruct((2, 16 * HD), F32),
        compiler_params=pltpu.CompilerParams(vmem_limit_bytes=8 << 20),
        name="merge_lower",
    )(parts, own_q, ancestors)


def project_kernel(hidden_ref, terms_ref, gain_ref, wq_ref, wk_ref, wv_ref, res_ref, out_ref):
    residual = hidden_ref[...].astype(F32) + terms_ref[...]
    res_ref[...] = residual
    square = jnp.sum(residual * residual, axis=1, keepdims=True)
    coarse = square.astype(BF16).astype(F32)
    lane = lax.broadcasted_iota(jnp.int32, residual.shape, 1)
    squares = jnp.where(lane < 64, coarse, square - coarse).astype(BF16)
    scaled = (residual * gain_ref[...]).astype(BF16)
    q = contract(scaled, wq_ref[...], ((1,), (0,))).astype(BF16)
    k = contract(scaled, wk_ref[...], ((1,), (0,))).astype(BF16)
    v = contract(scaled, wv_ref[...], ((1,), (0,))).astype(BF16)
    tails = [k[:, :HD], squares, k[:, HD:], squares, v[:, :HD], squares, v[:, HD:], squares]
    for r in range(8):
        rows = slice(16 * r, 16 * r + 16)
        for j in range(GROUP):
            at = r * GROUP + j
            out_ref[at, 0:16, :] = q[rows, 2 * j * HD : (2 * j + 1) * HD]
            out_ref[at, 16:32, :] = q[rows, (2 * j + 1) * HD : (2 * j + 2) * HD]
            out_ref[at, 32:48, :] = tails[j][rows]


def project(hidden, terms, gain, wq, wk, wv):
    rows = hidden.shape[0]
    return pl.pallas_call(
        project_kernel,
        out_shape=(
            jax.ShapeDtypeStruct((rows, HD), F32),
            jax.ShapeDtypeStruct((rows // 2, 48, HD), BF16),
        ),
        compiler_params=pltpu.CompilerParams(vmem_limit_bytes=8 << 20),
        name="project",
    )(hidden, terms, gain, wq, wk, wv)


def retained_kernel(
    width, len_ref, g_ref, k_ref, v_ref, pos_ref, anc_ref, out_ref, blend_scr, stat_scr
):
    place = lax.axis_index(SEQ)
    request = place // GROUP
    leader = place % GROUP == 0
    length = len_ref[request]
    kept = (pos_ref[...] < length).astype(F32)
    row = lax.broadcasted_iota(jnp.int32, (HD, 2 * HD), 0)
    col = lax.broadcasted_iota(jnp.int32, (HD, 2 * HD), 1)
    doubled = (row == col // 2).astype(F32).astype(BF16)
    pick_odd = lax.broadcasted_iota(jnp.int32, (1, 2 * HD), 1) % 2 == 1
    kept = jnp.concatenate([kept, jnp.zeros((6, kept.shape[1]), F32)], axis=0).astype(BF16)
    limits = []
    for c in range(0, kept.shape[1], HD):
        wide = contract(kept[:, c : c + HD], doubled, ((1,), (0,)))
        limits.append(jnp.where(pick_odd, wide[1:2], wide[0:1]))
    usable = jnp.concatenate(limits, axis=1)
    tile = g_ref[1, 32:48, :].astype(F32)
    square = tile[:, 0:1] + tile[:, 64:65]
    inverse = lax.rsqrt(square / width + EPS)

    def up(j, at):
        return (g_ref[j, at : at + 16, :].astype(F32) * inverse).astype(BF16)

    def stacked(h):
        return jnp.concatenate(
            [up((8 * h + g) // 2, 16 * ((8 * h + g) % 2)) for g in range(8)], axis=0
        )

    zero = jnp.zeros((16, HD), BF16)
    queries = jnp.concatenate([stacked(0), stacked(1)], axis=1)

    def near(first, second):
        return jnp.concatenate(
            [jnp.concatenate([first, zero], axis=1), jnp.concatenate([zero, second], axis=1)],
            axis=0,
        )

    near_keys = near(up(0, 32), up(2, 32))
    near_values = near(up(4, 32), up(6, 32))
    far = contract(queries, head_halves(k_ref[...]), ((1,), (1,))) * SCALE2
    far = far + jnp.where(usable > 0.5, 0.0, MASKED)
    row_pick = (
        lax.broadcasted_iota(jnp.int32, (128, 16), 0) % 16
        == lax.broadcasted_iota(jnp.int32, (128, 16), 1)
    )
    col_pick = (
        lax.broadcasted_iota(jnp.int32, (16, 32), 1) % 16
        == lax.broadcasted_iota(jnp.int32, (16, 32), 0)
    )
    ancestry = anc_ref[request].astype(F32).astype(BF16)
    seen = contract(ancestry, col_pick.astype(F32).astype(BF16), ((1,), (0,)))
    seen = contract(row_pick.astype(F32).astype(BF16), seen.astype(BF16), ((1,), (0,)))
    close = contract(queries, near_keys, ((1,), (1,))) * SCALE2
    close = jnp.where((seen > 0.5) & leader, close, MASKED)
    second = lax.broadcasted_iota(jnp.int32, close.shape, 1) >= 16
    n0 = jnp.max(jnp.where(second, MASKED, close), axis=1, keepdims=True)
    n1 = jnp.max(jnp.where(second, close, MASKED), axis=1, keepdims=True)
    m0, m1, odd = pair_max(far)
    s0, s1 = shift_of(jnp.maximum(m0, n0)), shift_of(jnp.maximum(m1, n1))
    weights, l0, l1 = pair_weights(far, s0, s1, odd)
    close_w = jnp.exp2(close - jnp.where(second, s1, s0))
    l0 = l0 + jnp.sum(jnp.where(second, 0.0, close_w), axis=1, keepdims=True)
    l1 = l1 + jnp.sum(jnp.where(second, close_w, 0.0), axis=1, keepdims=True)
    blend = contract(weights, head_halves(v_ref[...]), ((1,), (0,)))
    blend = blend + contract(close_w.astype(BF16), near_values, ((1,), (0,)))
    lane = lax.broadcasted_iota(jnp.int32, (128, HD), 1)
    stats = [jnp.where(lane < 64, s0, l0), jnp.where(lane < 64, s1, l1)]
    for h in range(2):
        for g in range(8):
            for half in range(2):
                at = 16 * g + 8 * half
                to = pl.ds(8 * half * 16 + 8 * h + g, 8, stride=16)
                blend_scr[to, :] = blend[at : at + 8, h * HD : (h + 1) * HD]
                stat_scr[to, :] = stats[h][at : at + 8]
    lane = lax.broadcasted_iota(jnp.int32, (16, HD), 1)
    for j in range(GROUP):
        out_ref[j, 0:32, :] = blend_scr[32 * j : 32 * j + 32, :].astype(BF16)
        out_ref[j, 32:48, :] = jnp.where(
            lane % 2 == 0, stat_scr[32 * j : 32 * j + 16, :], stat_scr[32 * j + 16 : 32 * j + 32, :]
        ).astype(BF16)


def retained_attend(width, lengths, gathered, keys, values, positions, ancestors):
    vmem = pl.BlockSpec(memory_space=pltpu.VMEM)
    return pl.pallas_call(
        functools.partial(retained_kernel, width),
        in_specs=[pl.BlockSpec(memory_space=pltpu.SMEM), vmem, vmem, vmem, vmem, vmem],
        out_specs=vmem,
        out_shape=jax.ShapeDtypeStruct((GROUP, 48, HD), BF16),
        scratch_shapes=[pltpu.VMEM((256, HD), F32), pltpu.VMEM((256, HD), F32)],
        compiler_params=pltpu.CompilerParams(vmem_limit_bytes=8 << 20),
        name="retained_attend",
    )(lengths, gathered, keys, values, positions, ancestors)


def finish_kernel(parts_ref, out_ref):
    stats = parts_ref[:, 32:48, :].astype(F32)
    highest = jnp.max(stats, axis=0)
    factor = jnp.exp2(jnp.minimum(stats - highest[None], 0.0))
    sums = pltpu.roll(stats.reshape(-1, HD), 64, 1).reshape(stats.shape)
    total = jnp.sum(sums * factor, axis=0)
    for i in range(2):
        rows = parts_ref[:, 16 * i : 16 * i + 16, :].astype(F32)
        blend = jnp.sum(rows * factor[:, :, i : i + 1], axis=0)
        heads = blend / total[:, i : i + 1]
        for c in range(16):
            out_ref[i : i + 1, c * HD : (c + 1) * HD] = heads[c : c + 1]


def finish_upper(parts):
    return pl.pallas_call(
        finish_kernel,
        out_shape=jax.ShapeDtypeStruct((2, 16 * HD), F32),
        name="finish_upper",
    )(parts)


def swapped(array, axis):
    return lax.ppermute(array, axis, [(0, 1), (1, 0)])


def shards(
    tree_hidden,
    query_low,
    key_tree_low,
    value_tree_low,
    cache_keys,
    cache_values,
    cache_lengths,
    ancestors,
    out_weight,
    norm_gain,
    w_query_up,
    w_key_up,
    w_value_up,
    retained_keys,
    retained_values,
    retained_index,
):
    seq_count = lax.axis_size(SEQ)
    requests, cache_part, kv_heads, _ = cache_keys.shape
    kept = retained_keys.shape[1]
    width = tree_hidden.shape[1] * seq_count
    own_q = query_low.reshape(2, 2, 8, HD).transpose(1, 0, 2, 3).reshape(32, HD)
    kv_own = jnp.concatenate(
        [
            key_tree_low.reshape(2, 2, HD).transpose(1, 0, 2).reshape(4, HD),
            value_tree_low.reshape(2, 2, HD).transpose(1, 0, 2).reshape(4, HD),
        ],
        axis=0,
    )
    queries = spread(own_q, SEQ)
    turned_keys = turn(cache_keys.reshape(requests, cache_part * kv_heads, HD))
    parts = cache_attend(
        cache_lengths,
        queries,
        turned_keys,
        cache_values.reshape(requests, cache_part * kv_heads, HD),
        kv_own,
    )
    own_heads = merge_lower(exchanged(parts, SEQ), own_q, ancestors)
    lower_all = spread(own_heads.astype(BF16), SEQ).reshape(2 * seq_count, -1)
    terms = jnp.dot(lower_all, out_weight, preferred_element_type=F32)
    terms = terms + swapped(terms, "c")
    terms = terms + swapped(terms, "yl")
    residual, projected = project(
        tree_hidden, terms, norm_gain.reshape(1, -1), w_query_up, w_key_up, w_value_up
    )
    summed = jnp.sum(exchanged(projected, SEQ).astype(F32), axis=0).astype(BF16)
    gathered = spread(summed, TEAM)
    upper = retained_attend(
        width,
        cache_lengths,
        gathered,
        retained_keys.reshape(kept * kv_heads, HD),
        retained_values.reshape(kept * kv_heads, HD),
        retained_index[0].T,
        ancestors,
    )
    upper_heads = finish_upper(exchanged(upper, TEAM))
    return (residual, upper_heads)


def solution(mesh):
    fine = Mesh(
        mesh.devices.reshape(4, 2, 4, 2, 2, 2), ("x", "zh", "zl", "yh", "yl", "c")
    )
    seq, tp = SEQ, ("yl", "c")
    return jax.shard_map(
        shards,
        mesh=fine,
        in_specs=(
            P(None, seq),
            P(seq, tp),
            P(seq, tp),
            P(seq, tp),
            P(None, seq, tp, None),
            P(None, seq, tp, None),
            P(),
            P(),
            P(tp, seq),
            P(seq),
            P(seq, tp),
            P(seq, tp),
            P(seq, tp),
            P(seq, None, tp, None),
            P(seq, None, tp, None),
            P(seq, None, tp),
        ),
        out_specs=(P(None, seq), P(seq, tp)),
        check_vma=False,
    )
```

time: 444 us -> 163 us (0.37)
  blocking collectives: 233 us -> 108 us
  waiting for transfers between devices: 101 us -> 18.7 us
  local copies, waits for them, and re-layouts: 43.5 us -> 4.16 us
  starting transfers between devices: 35.3 us -> 15.4 us
  other arithmetic: 17.4 us -> 0.18 us
  Pallas kernels: 0 us -> 14.3 us
  matrix products: 9.15 us -> 0.3 us
    all_gather x1 -> x0, blocking collectives: 187 us -> none  [in_one_piece(): filled = lax.all_gather(both, axis, axis=dim, tiled=True)]
    all_to_all x3 -> x5, blocking collectives: 46.1 us -> 108 us  [exchanged(): return lax.all_to_all(blocks, axis, split_axis=0, concat_axis=0, tiled=True)]
    all_to_all x2 -> x1, waiting for transfers between devices: 69.4 us -> 14.5 us  [exchanged(): return lax.all_to_all(blocks, axis, split_axis=0, concat_axis=0, tiled=True)]
    dynamic_slice x25 -> x0, local copies, waits for them, and re-layouts: 27.5 us -> none  [the longest x24 27.5 us: shards(): lax.map(cache_request, (gathered_q.reshape(requests, node_count, row_widt...]
    ppermute x18 -> x2, waiting for transfers between devices: 31.4 us -> 4.16 us  [swapped(): return lax.ppermute(array, axis, [(0, 1), (1, 0)])]
    ppermute x18 -> x2, starting transfers between devices: 25.5 us -> 1.71 us  [swapped(): return lax.ppermute(array, axis, [(0, 1), (1, 0)])]
    pallas_call x0 -> x6, Pallas kernels: none -> 14.3 us  [the longest x1 7.16 us: cache_attend(): pl.pallas_call(cache_kernel, in_specs=[pl.BlockSpec(memory_space=pltpu.SM...]
    dot_general x26 -> x1, matrix products: 9.15 us -> 0.3 us  [shards(): terms = jnp.dot(lower_all, out_weight, preferred_element_type=F32)]
  transfers between devices with their start and end apart: 20 -> 3, of which waited for: 15 -> 3; matrix products, arithmetic and copies ran while one was open for 1% -> 0% of each run, Pallas kernels for 0% -> 2%
where the time goes in v1:
time: 163 us; the launch traced here: 162 us
  blocking collectives  108 us (66%)
  waiting for transfers between devices  18.7 us (11%)
  starting transfers between devices  15.4 us (9%)
  Pallas kernels  14.3 us (9%)
  local copies, waits for them, and re-layouts  4.16 us (3%)
    all_to_all x5, blocking collectives, exchanged(): return lax.all_to_all(blocks, axis, split_axis=0, concat_axis=0, tiled=True)  108 us
    all_to_all x1, waiting for transfers between devices, exchanged(): return lax.all_to_all(blocks, axis, split_axis=0, concat_axis=0, tiled=True)  14.5 us
    all_to_all x1, starting transfers between devices, exchanged(): return lax.all_to_all(blocks, axis, split_axis=0, concat_axis=0, tiled=True)  13.7 us
    pallas_call x1, Pallas kernels, cache_attend(): pl.pallas_call(cache_kernel, in_specs=[pl.BlockSpec(memory_space=pltpu.SM...  7.16 us
    ppermute x2, waiting for transfers between devices, swapped(): return lax.ppermute(array, axis, [(0, 1), (1, 0)])  4.16 us
  transfers between devices with their start and end apart: 3, of which 3 were waited for; matrix products, arithmetic and copies ran while one was open for 0% of the time, Pallas kernels for 2%

profile of v1, /device:TPU:8, one launch (start us, length us, event | category | flops | bytes accessed | tf_op | source)
XLA Modules:
  0.0 162.2 jit_solution(12592977207809554185)
XLA Ops:
  0.6 0.8 copy.23
  1.4 0.9 broadcast_in_dim.9
  2.3 13.7 %all-to-all-start = ((bf16[64,32,128]{2,1,0:T(8,128)(2,1)}), bf16[64,32,128]{2,1,0:T(8,128)(2,1)S(1)}, u32[]{:S(2)}, u32[]{:S(2)}) async-start(bf16[64,32,128]{2,1,0:T(8,128)(2,1)} %broadcast_in_dim.9), calls=%async_computation | async-start | bytes 1048576 | tf_op jit(solution)/shard_map/all_to_all | solution.py:29
  16.0 2.6 %turn.1.kt_hbm = bf16[8,128,2048]{2,1,0:T(8,128)(2,1)S(1)} custom-call(bf16[8,2048,128]{2,1,0:T(8,128)(2,1)} %bitcast.34), custom_call_target="tpu_custom_call" | custom-call | tf_op jit(solution)/shard_map/turn/pallas_call | solution.py:101
  18.7 2.0 %copy-done.1 = bf16[8,128,2048]{2,1,0:T(8,128)(2,1)} copy-done((bf16[8,128,2048]{2,1,0:T(8,128)(2,1)}, bf16[8,128,2048]{2,1,0:T(8,128)(2,1)S(1)}, u32[]{:S(2)}) %copy-start.1) | copy-done | bytes 4194328
  20.6 14.5 %all-to-all-done.q_ref = bf16[64,32,128]{2,1,0:T(8,128)(2,1)S(1)} async-done(((bf16[64,32,128]{2,1,0:T(8,128)(2,1)}), bf16[64,32,128]{2,1,0:T(8,128)(2,1)S(1)}, u32[]{:S(2)}, u32[]{:S(2)}) %all-to-all-start) | async-done | bytes 524320 | tf_op jit(solution)/shard_map/all_to_all | solution.py:29
  35.1 7.2 %cache_attend.1 = bf16[64,48,128]{2,1,0:T(8,128)(2,1)S(1)} custom-call(s32[8]{0:T(128)S(1)} %copy-done.10, bf16[64,32,128]{2,1,0:T(8,128)(2,1)S(1)} %all-to-all-done.q_ref, bf16[8,128,2048]{2,1,0:T(8,128)(2,1)} %copy-done.1, bf16[8,2048,128]{2,1,0:T(8,128)(2,1)} %bitcast.35, bf16[8,128]{1,0:T(8,128)(2,1)S(1)} %pad_maximum_fusion.kv_ref), custom_call_target="tpu_custom_call" | custom-call | tf_op jit(solution)/shard_map/cache_attend/pallas_call | solution.py:199
  42.4 30.3 %all_to_all.30.parts_ref = bf16[64,48,128]{2,1,0:T(8,128)(2,1)S(1)} all-to-all(bf16[64,48,128]{2,1,0:T(8,128)(2,1)S(1)} %cache_attend.1), channel_id=1, replica_groups=mesh['x'=4,'zh'=2,'zl'=4,'yh'=2,'yl'=2,'c'=2] {'x','zh','zl','yh'}, dimensions={0} | all-to-all | bytes 1572864 | tf_op jit(solution)/shard_map/all_to_all | solution.py:29
  72.7 0.6 merge_lower.1
  73.3 0.3 broadcast_in_dim.10
  73.6 24.3 %all_to_all.31 = bf16[64,2,2048]{2,1,0:T(2,128)(2,1)S(1)} all-to-all(bf16[64,2,2048]{2,1,0:T(2,128)(2,1)S(1)} %broadcast_in_dim.10), channel_id=1, replica_groups=mesh['x'=4,'zh'=2,'zl'=4,'yh'=2,'yl'=2,'c'=2] {'x','zh','zl','yh'}, dimensions={0} | all-to-all | bytes 1048576 | tf_op jit(solution)/shard_map/all_to_all | solution.py:29
  97.9 0.2 reshape.48
  98.1 0.3 fusion
  98.4 0.1 collective-permute-start
  98.5 1.2 collective-permute-done
  99.8 1.6 collective-permute-start.1
  101.4 2.9 %collective-permute-done.1 = f32[128,128]{1,0:T(8,128)S(1)} collective-permute-done((f32[128,128]{1,0:T(8,128)S(1)}, f32[128,128]{1,0:T(8,128)S(1)}, u32[]{:S(2)}, u32[]{:S(2)}) %collective-permute-start.1) | collective-permute-done | bytes 65568 | tf_op jit(solution)/shard_map/ppermute | solution.py:445
  104.4 0.8 project.1
  105.1 29.5 %all_to_all.32 = bf16[64,48,128]{2,1,0:T(8,128)(2,1)S(1)} all-to-all(bf16[64,48,128]{2,1,0:T(8,128)(2,1)S(1)} %get-tuple-element.5), channel_id=1, replica_groups=mesh['x'=4,'zh'=2,'zl'=4,'yh'=2,'yl'=2,'c'=2] {'x','zh','zl','yh'}, dimensions={0} | all-to-all | bytes 1572864 | tf_op jit(solution)/shard_map/all_to_all | solution.py:29
  134.7 0.1 reduce_sum.12
  134.8 12.4 %all_to_all.33.g_ref = bf16[8,48,128]{2,1,0:T(8,128)(2,1)S(1)} all-to-all(bf16[8,48,128]{2,1,0:T(8,128)(2,1)S(1)} %broadcast_in_dim.11), channel_id=1, replica_groups=mesh['x'=4,'zh'=2,'zl'=4,'yh'=2,'yl'=2,'c'=2] {'zl','yh'}, dimensions={0} | all-to-all | bytes 196608 | tf_op jit(solution)/shard_map/all_to_all | solution.py:29
  147.2 1.5 retained_attend.1
  148.8 11.7 %all_to_all.34.parts_ref = bf16[8,48,128]{2,1,0:T(8,128)(2,1)} all-to-all(bf16[8,48,128]{2,1,0:T(8,128)(2,1)S(1)} %retained_attend.1), channel_id=1, replica_groups=mesh['x'=4,'zh'=2,'zl'=4,'yh'=2,'yl'=2,'c'=2] {'zl','yh'}, dimensions={0} | all-to-all | bytes 196608 | tf_op jit(solution)/shard_map/all_to_all | solution.py:29
  160.5 1.7 %finish_upper.1 = f32[2,2048]{1,0:T(2,128)} custom-call(bf16[8,48,128]{2,1,0:T(8,128)(2,1)} %all_to_all.34.parts_ref), custom_call_target="tpu_custom_call" | custom-call | tf_op jit(solution)/shard_map/finish_upper/pallas_call | solution.py:437
  (33 shorter events, 0.1 us)
Async XLA Ops:
  0.6 97.5 %copy-start = (bf16[2048,128]{1,0:T(8,128)(2,1)S(1)}, bf16[2048,128]{1,0:T(8,128)(2,1)}, u32[]{:S(2)}) copy-start(bf16[2048,128]{1,0:T(8,128)(2,1)} %param.24) | copy-start | bytes 1572868
  2.3 32.9 %all-to-all-start = ((bf16[64,32,128]{2,1,0:T(8,128)(2,1)}), bf16[64,32,128]{2,1,0:T(8,128)(2,1)S(1)}, u32[]{:S(2)}, u32[]{:S(2)}) async-start(bf16[64,32,128]{2,1,0:T(8,128)(2,1)} %broadcast_in_dim.9), calls=%async_computation | async-start | bytes 1048576 | tf_op jit(solution)/shard_map/all_to_all | solution.py:29
  16.0 4.7 %copy-start.12 = (bf16[2,256]{1,0:T(2,128)(2,1)S(1)}, bf16[2,256]{1,0:T(2,128)(2,1)}, u32[]{:S(2)}) copy-start(bf16[2,256]{1,0:T(2,128)(2,1)} %param.19) | copy-start | bytes 3076
  16.0 4.7 %copy-start.13 = (bf16[2,256]{1,0:T(2,128)(2,1)S(1)}, bf16[2,256]{1,0:T(2,128)(2,1)}, u32[]{:S(2)}) copy-start(bf16[2,256]{1,0:T(2,128)(2,1)} %param.18) | copy-start | bytes 3076
  16.0 19.2 %copy-start.10 = (s32[8]{0:T(128)S(1)}, s32[8]{0:T(128)}, u32[]{:S(2)}) copy-start(s32[8]{0:T(128)} %len_ref.3) | copy-start | bytes 100
  18.7 2.0 %copy-start.1 = (bf16[8,128,2048]{2,1,0:T(8,128)(2,1)}, bf16[8,128,2048]{2,1,0:T(8,128)(2,1)S(1)}, u32[]{:S(2)}) copy-start(bf16[8,128,2048]{2,1,0:T(8,128)(2,1)S(1)} %turn.1.kt_hbm) | copy-start | bytes 12582916
  35.1 37.6 %copy-start.5 = (s32[8,16,16]{2,1,0:T(8,128)S(1)}, s32[8,16,16]{2,1,0:T(8,128)}, u32[]{:S(2)}) copy-start(s32[8,16,16]{2,1,0:T(8,128)} %anc_ref.3) | copy-start | bytes 24580
  42.3 62.0 %copy-start.2 = (bf16[128,2048]{1,0:T(8,128)(2,1)S(1)}, bf16[128,2048]{1,0:T(8,128)(2,1)}, u32[]{:S(2)}) copy-start(bf16[128,2048]{1,0:T(8,128)(2,1)} %wq_ref.1) | copy-start | bytes 1572868
  42.3 62.0 %copy-start.6 = (bf16[128,256]{1,0:T(8,128)(2,1)S(1)}, bf16[128,256]{1,0:T(8,128)(2,1)}, u32[]{:S(2)}) copy-start(bf16[128,256]{1,0:T(8,128)(2,1)} %wk_ref.1) | copy-start | bytes 196612
  42.3 62.0 %copy-start.7 = (bf16[128,256]{1,0:T(8,128)(2,1)S(1)}, bf16[128,256]{1,0:T(8,128)(2,1)}, u32[]{:S(2)}) copy-start(bf16[128,256]{1,0:T(8,128)(2,1)} %wv_ref.1) | copy-start | bytes 196612
  42.3 62.0 %copy-start.8 = (bf16[128,128]{1,0:T(8,128)(2,1)S(1)}, bf16[128,128]{1,0:T(8,128)(2,1)}, u32[]{:S(2)}) copy-start(bf16[128,128]{1,0:T(8,128)(2,1)} %hidden_ref.1) | copy-start | bytes 98308
  42.4 62.0 %copy-start.11 = (f32[128]{0:T(128)S(1)}, f32[128]{0:T(128)}, u32[]{:S(2)}) copy-start(f32[128]{0:T(128)} %param.25) | copy-start | bytes 1540
  72.7 74.5 %copy-start.3 = (bf16[1,512,2,128]{3,2,1,0:T(2,128)(2,1)S(1)}, bf16[1,512,2,128]{3,2,1,0:T(2,128)(2,1)}, u32[]{:S(2)}) copy-start(bf16[1,512,2,128]{3,2,1,0:T(2,128)(2,1)} %param.29) | copy-start | bytes 786436
  72.7 74.5 %copy-start.4 = (bf16[1,512,2,128]{3,2,1,0:T(2,128)(2,1)S(1)}, bf16[1,512,2,128]{3,2,1,0:T(2,128)(2,1)}, u32[]{:S(2)}) copy-start(bf16[1,512,2,128]{3,2,1,0:T(2,128)(2,1)} %param.30) | copy-start | bytes 786436
  72.7 74.5 %copy-start.9 = (s32[1,512,2]{1,2,0:T(2,128)S(1)}, s32[1,512,2]{1,2,0:T(2,128)}, u32[]{:S(2)}) copy-start(s32[1,512,2]{1,2,0:T(2,128)} %param.31) | copy-start | bytes 12292
  98.4 1.3 collective-permute-start
  99.8 4.5 %collective-permute-start.1 = (f32[128,128]{1,0:T(8,128)S(1)}, f32[128,128]{1,0:T(8,128)S(1)}, u32[]{:S(2)}, u32[]{:S(2)}) collective-permute-start(f32[128,128]{1,0:T(8,128)S(1)} %add.6), channel_id=1, source_target_pairs={{0,2},{2,0},{1,3},{3,1},{4,6},{6,4},{5,7},{7,5},{8,10},{10,8},{9,1... | collective-permute-start | bytes 196616 | tf_op jit(solution)/shard_map/ppermute | solution.py:445

commit v2 on v1

--- a/solution.py
+++ b/solution.py
@@ -19,6 +19,9 @@
 
 SEQ = ("x", "zh", "zl", "yh")
 TEAM = ("zl", "yh")
+DEPTH = ("zh", "zl")
+FACE = ("x", "yh")
+SIDE = ("zh", "zl", "yh")
 
 
 def contract(a, b, dims):
@@ -131,16 +134,23 @@
     step = 256
     kv_own = kv_ref[...].astype(F32)
     odd = lax.broadcasted_iota(jnp.int32, (rows, HD), 1) % 2 == 1
-    lane = lax.broadcasted_iota(jnp.int32, (8, HD), 1)
+    lane = lax.broadcasted_iota(jnp.int32, (rows, HD), 1)
+    kept = {}
     column = lax.broadcasted_iota(jnp.int32, (1, step), 1)
     first_head = (column % 2 == 0).astype(F32).astype(BF16)
     second_head = (column % 2 == 1).astype(F32).astype(BF16)
 
     def score(r, scr):
-        block = q_ref[r * GROUP : (r + 1) * GROUP]
-        queries = jnp.concatenate(
-            [block[:, 0:16, :].reshape(rows, HD), block[:, 16:32, :].reshape(rows, HD)], axis=1
-        )
+        def half(h):
+            return jnp.concatenate(
+                [
+                    q_ref[2 * (r // 2) + j % 2, 4 * (r % 2) + j // 2, 16 * h : 16 * h + 16, :]
+                    for j in range(GROUP)
+                ],
+                axis=0,
+            )
+
+        queries = jnp.concatenate([half(0), half(1)], axis=1)
         limit = 2 * (len_ref[r] - start)
         folded = None
         for c in range(0, keys, step):
@@ -173,13 +183,26 @@
             )
         l0 = jnp.sum(jnp.where(odd, 0.0, total), axis=1, keepdims=True)
         l1 = jnp.sum(jnp.where(odd, total, 0.0), axis=1, keepdims=True)
-        stats = stat_tile(s0, s1, l0, l1)
-        for j in range(GROUP):
-            low, high, at = 16 * j, 16 * j + 16, r * GROUP + j
-            out_ref[at, 0:16, :] = mixed[low:high, 0:HD].astype(BF16)
-            out_ref[at, 16:32, :] = mixed[low:high, HD:].astype(BF16)
-            pair = jnp.where(lane % 2 == 0, stats[low : low + 8], stats[low + 8 : high])
-            out_ref[at, 32:48, :] = jnp.concatenate([pair, kv_own], axis=0).astype(BF16)
+        columns = jnp.where(
+            lane < 2, jnp.where(lane == 0, s0, l0), jnp.where(lane == 2, s1, l1)
+        )
+        kept[r] = columns.T
+        for h in range(2):
+            at = 2 * (r // 2) + h
+            low = 16 * GROUP * (r % 2)
+            out_ref[at, low : low + rows, :] = mixed[:, h * HD : (h + 1) * HD].astype(BF16)
+            if r % 2 == 1:
+                tile = jnp.concatenate(
+                    [
+                        kept[r - 1][2 * h : 2 * h + 2],
+                        kept[r][2 * h : 2 * h + 2],
+                        kv_own[2 * h : 2 * h + 2],
+                        kv_own[4 + 2 * h : 6 + 2 * h],
+                        jnp.zeros((8, HD), F32),
+                    ],
+                    axis=0,
+                )
+                out_ref[at, 2 * rows : 2 * rows + 16, :] = tile.astype(BF16)
 
     scratch = (first_scr, second_scr)
     fetch_keys(0).wait()
@@ -206,7 +229,7 @@
             vmem,
         ],
         out_specs=vmem,
-        out_shape=jax.ShapeDtypeStruct((requests * GROUP, 48, HD), BF16),
+        out_shape=jax.ShapeDtypeStruct((GROUP, 32 * GROUP + 16, HD), BF16),
         scratch_shapes=[
             pltpu.VMEM((16 * GROUP, count), F32),
             pltpu.VMEM((16 * GROUP, count), F32),
@@ -225,67 +248,138 @@
     )
 
 
-def merge_kernel(parts_ref, q_ref, anc_ref, out_ref):
-    place = lax.axis_index(SEQ)
-    request = place // GROUP
-    node = 2 * (place % GROUP)
-    first = pl.multiple_of(request * GROUP, GROUP)
-    tree = parts_ref[pl.ds(first, GROUP), 32:48, :].astype(F32)[:, 8:16, :].reshape(64, HD)
-    tree_values = pltpu.roll(tree, 60, 0)
-    tree_keys = tree.astype(BF16)
-    row = lax.broadcasted_iota(jnp.int32, (32, 64), 0)
-    col = lax.broadcasted_iota(jnp.int32, (32, 64), 1)
-    picks = (
-        lax.broadcasted_iota(jnp.int32, (16, 64), 0)
-        == 2 * (lax.broadcasted_iota(jnp.int32, (16, 64), 1) // 8)
-        + lax.broadcasted_iota(jnp.int32, (16, 64), 1) % 2
-    )
-    ancestry = contract(
-        anc_ref[request].astype(F32).astype(BF16), picks.astype(F32).astype(BF16), ((1,), (0,))
-    )
-    which = lax.broadcasted_iota(jnp.int32, (16, 64), 0)
-    mine0 = jnp.sum(jnp.where(which == node, ancestry, 0.0), axis=0, keepdims=True)
-    mine1 = jnp.sum(jnp.where(which == node + 1, ancestry, 0.0), axis=0, keepdims=True)
-    seen = jnp.where((row // 8) % 2 == 0, mine0, mine1)
-    allowed = (seen > 0.5) & ((col // 4) % 2 == 0) & ((col // 2) % 2 == row // 16)
-    scores = contract(q_ref[...], tree_keys, ((1,), (1,))) * SCALE2
-    scores = jnp.where(allowed, scores, MASKED)
-    m_tree = jnp.max(scores, axis=1, keepdims=True)
-    w_tree = jnp.where(allowed, jnp.exp2(scores - m_tree), 0.0)
-    l_tree = jnp.sum(w_tree, axis=1, keepdims=True)
-    o_tree = contract(w_tree.astype(BF16), tree_values.astype(BF16), ((1,), (0,)))
-
-    stats = parts_ref[:, 32:48, :].astype(F32)[:, 0:8, :]
+def folded_parts(parts_ref):
+    stats = parts_ref[:, 256:272, :].astype(F32)
     highest = jnp.max(stats, axis=0)
     factor = jnp.exp2(jnp.minimum(stats - highest[None], 0.0))
-    sums = pltpu.roll(stats.reshape(-1, HD), 64, 1).reshape(stats.shape)
-    total = jnp.sum(sums * factor, axis=0)
-    for h in range(2):
-        both = parts_ref[:, 16 * h : 16 * h + 16, :].astype(F32)
-        for i in range(2):
-            lane = h * 32 + i
-            at = 16 * h + 8 * i
-            blend = jnp.sum(both[:, 8 * i : 8 * i + 8, :] * factor[:, :, lane : lane + 1], axis=0)
-            m_far = highest[:, lane : lane + 1]
-            m_near = m_tree[at : at + 8]
-            top = jnp.maximum(m_far, m_near)
-            f_far = jnp.exp2(m_far - top)
-            f_near = jnp.exp2(m_near - top)
-            denominator = total[:, lane : lane + 1] * f_far + l_tree[at : at + 8] * f_near
-            heads = (blend * f_far + o_tree[at : at + 8] * f_near) / denominator
-            for g in range(8):
-                out_ref[i : i + 1, (8 * h + g) * HD : (8 * h + g + 1) * HD] = heads[g : g + 1]
-
-
-def merge_lower(parts, own_q, ancestors):
+    columns = factor.reshape(HD, HD).T
+    blends, sums = [], []
+    for r in range(2):
+        mixed = None
+        total = None
+        for source in range(GROUP):
+            at = 16 * source + 2 * r
+            part = parts_ref[source, HD * r : HD * r + HD, :].astype(F32) * columns[:, at : at + 1]
+            weight = stats[source, 2 * r + 1 : 2 * r + 2] * factor[source, 2 * r : 2 * r + 1]
+            mixed = part if mixed is None else mixed + part
+            total = weight if total is None else total + weight
+        blends.append(mixed)
+        sums.append(total)
+    return stats, highest, blends, sums
+
+
+def fold_kernel(parts_ref, out_ref):
+    _, highest, blends, sums = folded_parts(parts_ref)
+    out_ref[0:HD, :] = blends[0].astype(BF16)
+    out_ref[HD : 2 * HD, :] = blends[1].astype(BF16)
+    first = 2 * lax.axis_index("x")
+    tree0 = parts_ref[first, 256:272, :].astype(F32)[4:8]
+    tree1 = parts_ref[first + 1, 256:272, :].astype(F32)[4:8]
+    tile = jnp.concatenate(
+        [
+            highest[0:1],
+            sums[0],
+            highest[2:3],
+            sums[1],
+            tree0,
+            tree1,
+            jnp.zeros((4, HD), F32),
+        ],
+        axis=0,
+    )
+    out_ref[2 * HD : 2 * HD + 16, :] = tile.astype(BF16)
+
+
+def fold_parts(parts):
+    return pl.pallas_call(
+        fold_kernel,
+        in_specs=[pl.BlockSpec(memory_space=pltpu.VMEM)],
+        out_specs=pl.BlockSpec(memory_space=pltpu.VMEM),
+        out_shape=jax.ShapeDtypeStruct(parts.shape[1:], BF16),
+        compiler_params=pltpu.CompilerParams(vmem_limit_bytes=8 << 20),
+        name="fold_parts",
+    )(parts)
+
+
+def merge_kernel(parts_ref, q_ref, anc_ref, out_ref, scr):
+    x = lax.axis_index("x")
+    head = lax.axis_index("yh")
+    stats, highest, blends, sums = folded_parts(parts_ref)
+    padding = jnp.zeros((HD - 4, HD), F32)
+    turned = jnp.concatenate([highest[0:1], sums[0], highest[2:3], sums[1], padding], axis=0).T
+    entry = lax.broadcasted_iota(jnp.int32, (16, 64), 1)
+    inner = entry % 16 - 4
+    is_key = (inner >= 0) & (inner < 8) & (inner % 4 < 2)
+    node_of = (entry // 16) * 4 + (inner // 4) * 2 + inner % 4
+    pick = (is_key & (node_of == lax.broadcasted_iota(jnp.int32, (16, 64), 0))).astype(F32)
+    place = (
+        lax.broadcasted_iota(jnp.int32, (HD, 16), 0) // 8
+        == lax.broadcasted_iota(jnp.int32, (HD, 16), 1)
+    ).astype(F32)
+    for r in range(2):
+        tree = stats[4 * r : 4 * r + 4].reshape(64, HD)
+        values = pltpu.roll(tree, 62, 0).astype(BF16)
+        queries = jnp.concatenate(
+            [
+                jnp.where(
+                    head == 0,
+                    q_ref[2 * x + j % 2, 4 * r + j // 2, 0:16, :].astype(F32),
+                    q_ref[2 * x + j % 2, 4 * r + j // 2, 16:32, :].astype(F32),
+                )
+                for j in range(GROUP)
+            ],
+            axis=0,
+        ).astype(BF16)
+        ancestry = anc_ref[2 * x + r].astype(F32).astype(BF16)
+        seen = contract(ancestry, pick.astype(BF16), ((1,), (0,))).astype(BF16)
+        seen = contract(place.astype(BF16), seen, ((1,), (0,)))
+        scores = contract(queries, tree.astype(BF16), ((1,), (1,))) * SCALE2
+        scores = jnp.where(seen > 0.5, scores, MASKED)
+        m_near = jnp.max(scores, axis=1, keepdims=True)
+        w_near = jnp.where(seen > 0.5, jnp.exp2(scores - m_near), 0.0)
+        l_near = jnp.sum(w_near, axis=1, keepdims=True)
+        o_near = contract(w_near.astype(BF16), values, ((1,), (0,)))
+        m_far = turned[:, 2 * r : 2 * r + 1]
+        top = jnp.maximum(m_far, m_near)
+        f_far = jnp.exp2(m_far - top)
+        f_near = jnp.exp2(m_near - top)
+        denominator = turned[:, 2 * r + 1 : 2 * r + 2] * f_far + l_near * f_near
+        scr[HD * r : HD * r + HD, :] = (blends[r] * f_far + o_near * f_near) / denominator
+    for g in range(8):
+        out_ref[:, g * HD : (g + 1) * HD] = scr[pl.ds(g, 32, stride=8), :].astype(BF16)
+
+
+def merge_lower(parts, queries, ancestors):
     return pl.pallas_call(
         merge_kernel,
         in_specs=[pl.BlockSpec(memory_space=pltpu.VMEM)] * 3,
         out_specs=pl.BlockSpec(memory_space=pltpu.VMEM),
-        out_shape=jax.ShapeDtypeStruct((2, 16 * HD), F32),
+        out_shape=jax.ShapeDtypeStruct((32, 8 * HD), BF16),
+        scratch_shapes=[pltpu.VMEM((2 * HD, HD), F32)],
         compiler_params=pltpu.CompilerParams(vmem_limit_bytes=8 << 20),
         name="merge_lower",
-    )(parts, own_q, ancestors)
+    )(parts, queries, ancestors)
+
+
+def output_kernel(heads_ref, weight_ref, out_ref):
+    half = weight_ref.shape[0] // 2
+    total = None
+    for h in range(2):
+        rows = jnp.concatenate([heads_ref[2 * x + h] for x in range(4)], axis=0)
+        term = contract(rows, weight_ref[h * half : (h + 1) * half, :], ((1,), (0,)))
+        total = term if total is None else total + term
+    out_ref[...] = total
+
+
+def output_terms(heads, weight):
+    return pl.pallas_call(
+        output_kernel,
+        in_specs=[pl.BlockSpec(memory_space=pltpu.VMEM)] * 2,
+        out_specs=pl.BlockSpec(memory_space=pltpu.VMEM),
+        out_shape=jax.ShapeDtypeStruct((4 * heads.shape[1], weight.shape[1]), F32),
+        compiler_params=pltpu.CompilerParams(vmem_limit_bytes=8 << 20),
+        name="output_terms",
+    )(heads, weight)
 
 
 def project_kernel(hidden_ref, terms_ref, gain_ref, wq_ref, wk_ref, wv_ref, res_ref, out_ref):
@@ -299,14 +393,13 @@
     q = contract(scaled, wq_ref[...], ((1,), (0,))).astype(BF16)
     k = contract(scaled, wk_ref[...], ((1,), (0,))).astype(BF16)
     v = contract(scaled, wv_ref[...], ((1,), (0,))).astype(BF16)
-    tails = [k[:, :HD], squares, k[:, HD:], squares, v[:, :HD], squares, v[:, HD:], squares]
-    for r in range(8):
-        rows = slice(16 * r, 16 * r + 16)
-        for j in range(GROUP):
-            at = r * GROUP + j
-            out_ref[at, 0:16, :] = q[rows, 2 * j * HD : (2 * j + 1) * HD]
-            out_ref[at, 16:32, :] = q[rows, (2 * j + 1) * HD : (2 * j + 2) * HD]
-            out_ref[at, 32:48, :] = tails[j][rows]
+    for h in range(2):
+        blocks = [q[:, (8 * h + g) * HD : (8 * h + g + 1) * HD] for g in range(8)]
+        blocks += [k[:, h * HD : (h + 1) * HD], v[:, h * HD : (h + 1) * HD], squares]
+        for r in range(8):
+            for b, block in enumerate(blocks):
+                at = (r % 2) * 176 + 16 * b
+                out_ref[2 * (r // 2) + h, at : at + 16, :] = block[16 * r : 16 * r + 16]
 
 
 def project(hidden, terms, gain, wq, wk, wv):
@@ -315,7 +408,7 @@
         project_kernel,
         out_shape=(
             jax.ShapeDtypeStruct((rows, HD), F32),
-            jax.ShapeDtypeStruct((rows // 2, 48, HD), BF16),
+            jax.ShapeDtypeStruct((GROUP, 352, HD), BF16),
         ),
         compiler_params=pltpu.CompilerParams(vmem_limit_bytes=8 << 20),
         name="project",
@@ -340,17 +433,20 @@
         wide = contract(kept[:, c : c + HD], doubled, ((1,), (0,)))
         limits.append(jnp.where(pick_odd, wide[1:2], wide[0:1]))
     usable = jnp.concatenate(limits, axis=1)
-    tile = g_ref[1, 32:48, :].astype(F32)
-    square = tile[:, 0:1] + tile[:, 64:65]
+    raw = []
+    for h in range(2):
+        total = g_ref[h].astype(F32)
+        for z in range(1, GROUP):
+            total = total + g_ref[2 * z + h].astype(F32)
+        raw.append(total)
+    square = raw[0][160:176, 0:1] + raw[0][160:176, 64:65]
     inverse = lax.rsqrt(square / width + EPS)
 
-    def up(j, at):
-        return (g_ref[j, at : at + 16, :].astype(F32) * inverse).astype(BF16)
+    def up(h, b):
+        return (raw[h][16 * b : 16 * b + 16] * inverse).astype(BF16)
 
     def stacked(h):
-        return jnp.concatenate(
-            [up((8 * h + g) // 2, 16 * ((8 * h + g) % 2)) for g in range(8)], axis=0
-        )
+        return jnp.concatenate([up(h, g) for g in range(8)], axis=0)
 
     zero = jnp.zeros((16, HD), BF16)
     queries = jnp.concatenate([stacked(0), stacked(1)], axis=1)
@@ -361,8 +457,8 @@
             axis=0,
         )
 
-    near_keys = near(up(0, 32), up(2, 32))
-    near_values = near(up(4, 32), up(6, 32))
+    near_keys = near(up(0, 8), up(1, 8))
+    near_values = near(up(0, 9), up(1, 9))
     far = contract(queries, head_halves(k_ref[...]), ((1,), (1,))) * SCALE2
     far = far + jnp.where(usable > 0.5, 0.0, MASKED)
     row_pick = (
@@ -475,7 +571,7 @@
         ],
         axis=0,
     )
-    queries = spread(own_q, SEQ)
+    queries = spread(spread(own_q, DEPTH).reshape(-1, HD), FACE).reshape(GROUP, GROUP, 32, HD)
     turned_keys = turn(cache_keys.reshape(requests, cache_part * kv_heads, HD))
     parts = cache_attend(
         cache_lengths,
@@ -484,16 +580,17 @@
         cache_values.reshape(requests, cache_part * kv_heads, HD),
         kv_own,
     )
-    own_heads = merge_lower(exchanged(parts, SEQ), own_q, ancestors)
-    lower_all = spread(own_heads.astype(BF16), SEQ).reshape(2 * seq_count, -1)
-    terms = jnp.dot(lower_all, out_weight, preferred_element_type=F32)
+    folded = spread(fold_parts(exchanged(parts, FACE)), DEPTH)
+    heads = merge_lower(folded, queries, ancestors)
+    terms = output_terms(spread(heads, FACE), out_weight)
     terms = terms + swapped(terms, "c")
     terms = terms + swapped(terms, "yl")
     residual, projected = project(
         tree_hidden, terms, norm_gain.reshape(1, -1), w_query_up, w_key_up, w_value_up
     )
-    summed = jnp.sum(exchanged(projected, SEQ).astype(F32), axis=0).astype(BF16)
-    gathered = spread(summed, TEAM)
+    summed = jnp.sum(exchanged(projected, FACE).astype(F32), axis=0).astype(BF16)
+    shares = jnp.broadcast_to(summed.reshape(2, 1, 176, HD), (2, GROUP, 176, HD))
+    gathered = exchanged(shares.reshape(2 * GROUP, 176, HD), SIDE)
     upper = retained_attend(
         width,
         cache_lengths,

time: 163 us -> 150 us (0.920)
  waiting for transfers between devices: 18.7 us -> 9.24 us
  starting transfers between devices: 15.4 us -> 7.56 us
  blocking collectives: 108 us -> 113 us
    all_to_all x1, waiting for transfers between devices: 14.5 us -> 5.08 us  [exchanged(): return lax.all_to_all(blocks, axis, split_axis=0, concat_axis=0, tiled=True)]
    all_to_all x1, starting transfers between devices: 13.7 us -> 6.03 us  [exchanged(): return lax.all_to_all(blocks, axis, split_axis=0, concat_axis=0, tiled=True)]
    all_to_all x5 -> x7, blocking collectives: 108 us -> 113 us  [exchanged(): return lax.all_to_all(blocks, axis, split_axis=0, concat_axis=0, tiled=True)]
where the time goes in v2:
time: 150 us
  blocking collectives  113 us (75%)
  Pallas kernels  15.7 us (10%)
  waiting for transfers between devices  9.24 us (6%)
  starting transfers between devices  7.56 us (5%)
  local copies, waits for them, and re-layouts  3.85 us (3%)
    all_to_all x7, blocking collectives, exchanged(): return lax.all_to_all(blocks, axis, split_axis=0, concat_axis=0, tiled=True)  113 us
    pallas_call x1, Pallas kernels, cache_attend(): pl.pallas_call(cache_kernel, in_specs=[pl.BlockSpec(memory_space=pltpu.SM...  7.08 us
    all_to_all x1, starting transfers between devices, exchanged(): return lax.all_to_all(blocks, axis, split_axis=0, concat_axis=0, tiled=True)  6.03 us
    all_to_all x1, waiting for transfers between devices, exchanged(): return lax.all_to_all(blocks, axis, split_axis=0, concat_axis=0, tiled=True)  5.08 us
    ppermute x2, waiting for transfers between devices, swapped(): return lax.ppermute(array, axis, [(0, 1), (1, 0)])  4.16 us
  transfers between devices with their start and end apart: 3, of which 3 were waited for; matrix products, arithmetic and copies ran while one was open for 0% of the time, Pallas kernels for 2%

profile of v2, /device:TPU:8, one launch (start us, length us, event | category | flops | bytes accessed | tf_op | source)
XLA Modules:
  0.0 149.9 jit_solution(9450740009481961757)
XLA Ops:
  0.6 0.7 copy.27
  1.4 16.6 %all_to_all.40 = bf16[8,32,128]{2,1,0:T(8,128)(2,1)S(1)} all-to-all(bf16[8,32,128]{2,1,0:T(8,128)(2,1)S(1)} %broadcast_in_dim.19), channel_id=1, replica_groups=mesh['x'=4,'zh'=2,'zl'=4,'yh'=2,'yl'=2,'c'=2] {'zh','zl'}, dimensions={0} | all-to-all | bytes 131072 | tf_op jit(solution)/shard_map/all_to_all | solution.py:32
  18.0 0.9 broadcast_in_dim.20
  18.9 6.0 %all-to-all-start.1 = ((bf16[8,256,128]{2,1,0:T(8,128)(2,1)}), bf16[8,256,128]{2,1,0:T(8,128)(2,1)S(1)}, u32[]{:S(2)}, u32[]{:S(2)}) async-start(bf16[8,256,128]{2,1,0:T(8,128)(2,1)} %broadcast_in_dim.20), calls=%async_computation.1 | async-start | bytes 1048576 | tf_op jit(solution)/shard_map/all_to_all | solution.py:32
  24.9 2.7 %turn.1.kt_hbm = bf16[8,128,2048]{2,1,0:T(8,128)(2,1)S(1)} custom-call(bf16[8,2048,128]{2,1,0:T(8,128)(2,1)} %bitcast.37), custom_call_target="tpu_custom_call" | custom-call | tf_op jit(solution)/shard_map/turn/pallas_call | solution.py:104
  27.6 2.0 %copy-done = bf16[8,128,2048]{2,1,0:T(8,128)(2,1)} copy-done((bf16[8,128,2048]{2,1,0:T(8,128)(2,1)}, bf16[8,128,2048]{2,1,0:T(8,128)(2,1)S(1)}, u32[]{:S(2)}) %copy-start) | copy-done | bytes 4194328
  29.6 5.1 %all-to-all-done.1 = bf16[8,256,128]{2,1,0:T(8,128)(2,1)S(1)} async-done(((bf16[8,256,128]{2,1,0:T(8,128)(2,1)}), bf16[8,256,128]{2,1,0:T(8,128)(2,1)S(1)}, u32[]{:S(2)}, u32[]{:S(2)}) %all-to-all-start.1) | async-done | bytes 524320 | tf_op jit(solution)/shard_map/all_to_all | solution.py:32
  34.7 7.1 %cache_attend.1 = bf16[8,272,128]{2,1,0:T(8,128)(2,1)S(1)} custom-call(s32[8]{0:T(128)S(1)} %copy-done.10, bf16[8,8,32,128]{3,2,1,0:T(8,128)(2,1)S(1)} %bitcast.31, bf16[8,128,2048]{2,1,0:T(8,128)(2,1)} %copy-done, bf16[8,2048,128]{2,1,0:T(8,128)(2,1)} %bitcast.38, bf16[8,128]{1,0:T(8,128)(2,1)S(1)} %pad_maximum_fusion.kv_ref), custom_call_target="tpu_custom_call" | custom-call | tf_op jit(solution)/shard_map/cache_attend/pallas_call | solution.py:222
  41.8 13.6 %all_to_all.41.parts_ref = bf16[8,272,128]{2,1,0:T(8,128)(2,1)S(1)} all-to-all(bf16[8,272,128]{2,1,0:T(8,128)(2,1)S(1)} %cache_attend.1), channel_id=1, replica_groups=mesh['x'=4,'zh'=2,'zl'=4,'yh'=2,'yl'=2,'c'=2] {'x','yh'}, dimensions={0} | all-to-all | bytes 1114112 | tf_op jit(solution)/shard_map/all_to_all | solution.py:32
  55.5 0.5 fold_parts.1
  56.0 18.4 %all_to_all.42.parts_ref = bf16[8,272,128]{2,1,0:T(8,128)(2,1)S(1)} all-to-all(bf16[8,272,128]{2,1,0:T(8,128)(2,1)S(1)} %broadcast_in_dim.21), channel_id=1, replica_groups=mesh['x'=4,'zh'=2,'zl'=4,'yh'=2,'yl'=2,'c'=2] {'zh','zl'}, dimensions={0} | all-to-all | bytes 1114112 | tf_op jit(solution)/shard_map/all_to_all | solution.py:32
  74.5 1.3 merge_lower.1
  75.8 12.8 %all_to_all.43.heads_ref = bf16[8,32,1024]{2,1,0:T(8,128)(2,1)S(1)} all-to-all(bf16[8,32,1024]{2,1,0:T(8,128)(2,1)S(1)} %broadcast_in_dim.22), channel_id=1, replica_groups=mesh['x'=4,'zh'=2,'zl'=4,'yh'=2,'yl'=2,'c'=2] {'x','yh'}, dimensions={0} | all-to-all | bytes 1048576 | tf_op jit(solution)/shard_map/all_to_all | solution.py:32
  88.6 0.3 output_terms.1
  89.0 1.2 collective-permute-done
  90.2 1.4 collective-permute-start.1
  91.7 2.9 %collective-permute-done.1 = f32[128,128]{1,0:T(8,128)S(1)} collective-permute-done((f32[128,128]{1,0:T(8,128)S(1)}, f32[128,128]{1,0:T(8,128)S(1)}, u32[]{:S(2)}, u32[]{:S(2)}) %collective-permute-start.1) | collective-permute-done | bytes 65568 | tf_op jit(solution)/shard_map/ppermute | solution.py:541
  94.7 0.7 project.1
  95.3 15.5 %all_to_all.44 = bf16[8,352,128]{2,1,0:T(8,128)(2,1)S(1)} all-to-all(bf16[8,352,128]{2,1,0:T(8,128)(2,1)S(1)} %get-tuple-element.5), channel_id=1, replica_groups=mesh['x'=4,'zh'=2,'zl'=4,'yh'=2,'yl'=2,'c'=2] {'x','yh'}, dimensions={0} | all-to-all | bytes 1441792 | tf_op jit(solution)/shard_map/all_to_all | solution.py:32
  110.8 0.1 reduce_sum.12
  111.0 23.9 %all_to_all.45.g_ref = bf16[16,176,128]{2,1,0:T(8,128)(2,1)S(1)} all-to-all(bf16[16,176,128]{2,1,0:T(8,128)(2,1)S(1)} %bitcast.39), channel_id=1, replica_groups=mesh['x'=4,'zh'=2,'zl'=4,'yh'=2,'yl'=2,'c'=2] {'zh','zl','yh'}, dimensions={0} | all-to-all | bytes 1441792 | tf_op jit(solution)/shard_map/all_to_all | solution.py:32
  135.0 1.6 %retained_attend.1 = bf16[8,48,128]{2,1,0:T(8,128)(2,1)S(1)} custom-call(s32[8]{0:T(128)S(1)} %copy-done.10, bf16[16,176,128]{2,1,0:T(8,128)(2,1)S(1)} %all_to_all.45.g_ref, bf16[1024,128]{1,0:T(8,128)(2,1)S(1)} %bitcast.33, bf16[1024,128]{1,0:T(8,128)(2,1)S(1)} %bitcast.34, s32[2,512]{1,0:T(2,128)S(1)} %bitcast.35, s32[8,16,16]{2,1,0:T(8,128)S(1)} %copy-done.5), custom_call_target="tpu_custom_call" | custom-call | tf_op jit(solution)/shard_map/retained_attend/pallas_call | solution.py:507
  136.5 11.7 %all_to_all.46.parts_ref = bf16[8,48,128]{2,1,0:T(8,128)(2,1)} all-to-all(bf16[8,48,128]{2,1,0:T(8,128)(2,1)S(1)} %retained_attend.1), channel_id=1, replica_groups=mesh['x'=4,'zh'=2,'zl'=4,'yh'=2,'yl'=2,'c'=2] {'zl','yh'}, dimensions={0} | all-to-all | bytes 196608 | tf_op jit(solution)/shard_map/all_to_all | solution.py:32
  148.2 1.7 %finish_upper.1 = f32[2,2048]{1,0:T(2,128)} custom-call(bf16[8,48,128]{2,1,0:T(8,128)(2,1)} %all_to_all.46.parts_ref), custom_call_target="tpu_custom_call" | custom-call | tf_op jit(solution)/shard_map/finish_upper/pallas_call | solution.py:533
  (36 shorter events, 0.4 us)
Async XLA Ops:
  18.9 15.8 %all-to-all-start.1 = ((bf16[8,256,128]{2,1,0:T(8,128)(2,1)}), bf16[8,256,128]{2,1,0:T(8,128)(2,1)S(1)}, u32[]{:S(2)}, u32[]{:S(2)}) async-start(bf16[8,256,128]{2,1,0:T(8,128)(2,1)} %broadcast_in_dim.20), calls=%async_computation.1 | async-start | bytes 1048576 | tf_op jit(solution)/shard_map/all_to_all | solution.py:32
  24.9 4.7 %copy-start.12 = (bf16[2,256]{1,0:T(2,128)(2,1)S(1)}, bf16[2,256]{1,0:T(2,128)(2,1)}, u32[]{:S(2)}) copy-start(bf16[2,256]{1,0:T(2,128)(2,1)} %param.19) | copy-start | bytes 3076
  24.9 4.7 %copy-start.13 = (bf16[2,256]{1,0:T(2,128)(2,1)S(1)}, bf16[2,256]{1,0:T(2,128)(2,1)}, u32[]{:S(2)}) copy-start(bf16[2,256]{1,0:T(2,128)(2,1)} %param.18) | copy-start | bytes 3076
  24.9 9.7 %copy-start.10 = (s32[8]{0:T(128)S(1)}, s32[8]{0:T(128)}, u32[]{:S(2)}) copy-start(s32[8]{0:T(128)} %len_ref.3) | copy-start | bytes 100
  27.6 2.0 %copy-start = (bf16[8,128,2048]{2,1,0:T(8,128)(2,1)}, bf16[8,128,2048]{2,1,0:T(8,128)(2,1)S(1)}, u32[]{:S(2)}) copy-start(bf16[8,128,2048]{2,1,0:T(8,128)(2,1)S(1)} %turn.1.kt_hbm) | copy-start | bytes 12582916
  34.7 39.8 %copy-start.5 = (s32[8,16,16]{2,1,0:T(8,128)S(1)}, s32[8,16,16]{2,1,0:T(8,128)}, u32[]{:S(2)}) copy-start(s32[8,16,16]{2,1,0:T(8,128)} %anc_ref.3) | copy-start | bytes 24580
  41.7 46.8 %copy-start.2 = (bf16[2048,128]{1,0:T(8,128)(2,1)S(1)}, bf16[2048,128]{1,0:T(8,128)(2,1)}, u32[]{:S(2)}) copy-start(bf16[2048,128]{1,0:T(8,128)(2,1)} %weight_ref.1) | copy-start | bytes 1572868
  41.8 52.9 %copy-start.1 = (bf16[128,2048]{1,0:T(8,128)(2,1)S(1)}, bf16[128,2048]{1,0:T(8,128)(2,1)}, u32[]{:S(2)}) copy-start(bf16[128,2048]{1,0:T(8,128)(2,1)} %wq_ref.1) | copy-start | bytes 1572868
  41.8 52.9 %copy-start.6 = (bf16[128,256]{1,0:T(8,128)(2,1)S(1)}, bf16[128,256]{1,0:T(8,128)(2,1)}, u32[]{:S(2)}) copy-start(bf16[128,256]{1,0:T(8,128)(2,1)} %wk_ref.1) | copy-start | bytes 196612
  41.8 52.8 %copy-start.7 = (bf16[128,256]{1,0:T(8,128)(2,1)S(1)}, bf16[128,256]{1,0:T(8,128)(2,1)}, u32[]{:S(2)}) copy-start(bf16[128,256]{1,0:T(8,128)(2,1)} %wv_ref.1) | copy-start | bytes 196612
  41.8 52.8 %copy-start.8 = (bf16[128,128]{1,0:T(8,128)(2,1)S(1)}, bf16[128,128]{1,0:T(8,128)(2,1)}, u32[]{:S(2)}) copy-start(bf16[128,128]{1,0:T(8,128)(2,1)} %hidden_ref.1) | copy-start | bytes 98308
  41.8 52.8 %copy-start.11 = (f32[128]{0:T(128)S(1)}, f32[128]{0:T(128)}, u32[]{:S(2)}) copy-start(f32[128]{0:T(128)} %param.25) | copy-start | bytes 1540
  75.7 59.2 %copy-start.3 = (bf16[1,512,2,128]{3,2,1,0:T(2,128)(2,1)S(1)}, bf16[1,512,2,128]{3,2,1,0:T(2,128)(2,1)}, u32[]{:S(2)}) copy-start(bf16[1,512,2,128]{3,2,1,0:T(2,128)(2,1)} %param.29) | copy-start | bytes 786436
  75.7 59.2 %copy-start.4 = (bf16[1,512,2,128]{3,2,1,0:T(2,128)(2,1)S(1)}, bf16[1,512,2,128]{3,2,1,0:T(2,128)(2,1)}, u32[]{:S(2)}) copy-start(bf16[1,512,2,128]{3,2,1,0:T(2,128)(2,1)} %param.30) | copy-start | bytes 786436
  75.7 59.2 %copy-start.9 = (s32[1,512,2]{1,2,0:T(2,128)S(1)}, s32[1,512,2]{1,2,0:T(2,128)}, u32[]{:S(2)}) copy-start(s32[1,512,2]{1,2,0:T(2,128)} %param.31) | copy-start | bytes 12292
  88.9 1.3 collective-permute-start
  90.2 4.4 %collective-permute-start.1 = (f32[128,128]{1,0:T(8,128)S(1)}, f32[128,128]{1,0:T(8,128)S(1)}, u32[]{:S(2)}, u32[]{:S(2)}) collective-permute-start(f32[128,128]{1,0:T(8,128)S(1)} %add.6), channel_id=1, source_target_pairs={{0,2},{2,0},{1,3},{3,1},{4,6},{6,4},{5,7},{7,5},{8,10},{10,8},{9,1... | collective-permute-start | bytes 196616 | tf_op jit(solution)/shard_map/ppermute | solution.py:541

commit v3 on v2

--- a/solution.py
+++ b/solution.py
@@ -21,7 +21,6 @@
 TEAM = ("zl", "yh")
 DEPTH = ("zh", "zl")
 FACE = ("x", "yh")
-SIDE = ("zh", "zl", "yh")
 
 
 def contract(a, b, dims):
@@ -48,55 +47,29 @@
     return jnp.concatenate([first, second], axis=1)
 
 
-def pair_max(scores):
-    width = scores.shape[1]
-    folded = scores[:, 0:HD]
-    for c in range(HD, width, HD):
-        folded = jnp.maximum(folded, scores[:, c : c + HD])
-    odd = lax.broadcasted_iota(jnp.int32, folded.shape, 1) % 2 == 1
-    m0 = jnp.max(jnp.where(odd, MASKED, folded), axis=1, keepdims=True)
-    m1 = jnp.max(jnp.where(odd, folded, MASKED), axis=1, keepdims=True)
-    return m0, m1, odd
-
-
 def shift_of(maximum):
     return jnp.maximum(maximum, FLOOR).astype(BF16).astype(F32)
 
 
-def pair_weights(scores, s0, s1, odd):
-    width = scores.shape[1]
-    shift = jnp.where(odd, s1, s0)
-    pieces = []
-    total = jnp.zeros((scores.shape[0], HD), F32)
-    for c in range(0, width, HD):
-        w = jnp.exp2(scores[:, c : c + HD] - shift)
-        total = total + w
-        pieces.append(w.astype(BF16))
-    l0 = jnp.sum(jnp.where(odd, 0.0, total), axis=1, keepdims=True)
-    l1 = jnp.sum(jnp.where(odd, total, 0.0), axis=1, keepdims=True)
-    return jnp.concatenate(pieces, axis=1), l0, l1
-
-
-def stat_tile(s0, s1, l0, l1):
-    lane = lax.broadcasted_iota(jnp.int32, (s0.shape[0], HD), 1)
-    return jnp.where(
-        lane < 64, jnp.where(lane < 32, s0, s1), jnp.where(lane < 96, l0, l1)
-    )
-
-
-def turn_kernel(k_hbm, kt_ref, k_buf, sems):
+def turn_kernel(k_hbm, kt_hbm, k_buf, kt_buf, sems):
     requests, keys, _ = k_buf.shape
     step = 256
 
-    def copy(r):
-        return pltpu.make_async_copy(k_hbm.at[r], k_buf.at[r], sems.at[r])
+    def fetch(r):
+        return pltpu.make_async_copy(k_hbm.at[r], k_buf.at[r], sems.at[0, r])
+
+    def store(r):
+        return pltpu.make_async_copy(kt_buf.at[r], kt_hbm.at[r], sems.at[1, r])
 
     for r in range(requests):
-        copy(r).start()
+        fetch(r).start()
     for r in range(requests):
-        copy(r).wait()
+        fetch(r).wait()
         for c in range(0, keys, step):
-            kt_ref[r, :, c : c + step] = k_buf[r, c : c + step, :].T
+            kt_buf[r, :, c : c + step] = k_buf[r, c : c + step, :].T
+        store(r).start()
+    for r in range(requests):
+        store(r).wait()
 
 
 def turn(keys):
@@ -104,13 +77,14 @@
     return pl.pallas_call(
         turn_kernel,
         in_specs=[pl.BlockSpec(memory_space=pltpu.HBM)],
-        out_specs=pl.BlockSpec(memory_space=pltpu.VMEM),
-        out_shape=jax.ShapeDtypeStruct((requests, HD, count), BF16),
+        out_specs=pl.BlockSpec(memory_space=pltpu.HBM),
+        out_shape=pltpu.HBM((requests, HD, count), BF16),
         scratch_shapes=[
             pltpu.VMEM((requests, count, HD), BF16),
-            pltpu.SemaphoreType.DMA((requests,)),
+            pltpu.VMEM((requests, HD, count), BF16),
+            pltpu.SemaphoreType.DMA((2, requests)),
         ],
-        compiler_params=pltpu.CompilerParams(vmem_limit_bytes=8 << 20),
+        compiler_params=pltpu.CompilerParams(vmem_limit_bytes=12 << 20),
         name="turn",
     )(pltpu.with_memory_space_constraint(keys, pltpu.HBM))
 
@@ -415,118 +389,136 @@
     )(hidden, terms, gain, wq, wk, wv)
 
 
-def retained_kernel(
-    width, len_ref, g_ref, k_ref, v_ref, pos_ref, anc_ref, out_ref, blend_scr, stat_scr
-):
-    place = lax.axis_index(SEQ)
-    request = place // GROUP
-    leader = place % GROUP == 0
-    length = len_ref[request]
+def split_kernel(len_ref, k_ref, v_ref, pos_ref, mine_ref, give_ref):
+    own = lax.axis_index("yh")
+    length = len_ref[lax.axis_index(SEQ) // GROUP]
+    row = lax.broadcasted_iota(jnp.int32, (2 * HD, 2 * HD), 0)
+    col = lax.broadcasted_iota(jnp.int32, (2 * HD, 2 * HD), 1)
+    source = 2 * (row % HD) + jnp.where(row < HD, own, 1 - own)
+    pick = (col == source).astype(F32).astype(BF16)
+    count = k_ref.shape[0] // 2
+    for at, ref in ((0, k_ref), (count, v_ref)):
+        for c in range(0, count, HD):
+            pair = contract(pick, ref[2 * c : 2 * c + 2 * HD, :], ((1,), (0,))).astype(BF16)
+            mine_ref[at + c : at + c + HD, :] = pair[0:HD]
+            give_ref[at + c : at + c + HD, :] = pair[HD:]
     kept = (pos_ref[...] < length).astype(F32)
-    row = lax.broadcasted_iota(jnp.int32, (HD, 2 * HD), 0)
-    col = lax.broadcasted_iota(jnp.int32, (HD, 2 * HD), 1)
-    doubled = (row == col // 2).astype(F32).astype(BF16)
-    pick_odd = lax.broadcasted_iota(jnp.int32, (1, 2 * HD), 1) % 2 == 1
-    kept = jnp.concatenate([kept, jnp.zeros((6, kept.shape[1]), F32)], axis=0).astype(BF16)
-    limits = []
-    for c in range(0, kept.shape[1], HD):
-        wide = contract(kept[:, c : c + HD], doubled, ((1,), (0,)))
-        limits.append(jnp.where(pick_odd, wide[1:2], wide[0:1]))
-    usable = jnp.concatenate(limits, axis=1)
-    raw = []
-    for h in range(2):
-        total = g_ref[h].astype(F32)
-        for z in range(1, GROUP):
-            total = total + g_ref[2 * z + h].astype(F32)
-        raw.append(total)
-    square = raw[0][160:176, 0:1] + raw[0][160:176, 64:65]
+    rows0 = [kept[0:1, c : c + HD] for c in range(0, count, HD)]
+    rows1 = [kept[1:2, c : c + HD] for c in range(0, count, HD)]
+    rest = jnp.zeros((16 - len(rows0), HD), F32)
+    limits0 = jnp.concatenate(rows0 + [rest], axis=0)
+    limits1 = jnp.concatenate(rows1 + [rest], axis=0)
+    mine_ref[2 * count : 2 * count + 16, :] = jnp.where(own == 0, limits0, limits1).astype(BF16)
+    give_ref[2 * count : 2 * count + 16, :] = jnp.where(own == 0, limits1, limits0).astype(BF16)
+
+
+def split_heads(lengths, keys, values, positions):
+    count = keys.shape[0]
+    vmem = pl.BlockSpec(memory_space=pltpu.VMEM)
+    return pl.pallas_call(
+        split_kernel,
+        in_specs=[pl.BlockSpec(memory_space=pltpu.SMEM), vmem, vmem, vmem],
+        out_specs=[vmem, vmem],
+        out_shape=[jax.ShapeDtypeStruct((count + 16, HD), BF16)] * 2,
+        compiler_params=pltpu.CompilerParams(vmem_limit_bytes=8 << 20),
+        name="split_heads",
+    )(lengths, keys, values, positions)
+
+
+def retained_kernel(width, sum_ref, mine_ref, other_ref, anc_ref, out_ref, blend_scr, stat_scr):
+    request = lax.axis_index(SEQ) // GROUP
+    leader = lax.axis_index("zl") == 0
+    raw = sum_ref[...].astype(F32)
+    square = raw[160:176, 0:1] + raw[160:176, 64:65]
     inverse = lax.rsqrt(square / width + EPS)
 
-    def up(h, b):
-        return (raw[h][16 * b : 16 * b + 16] * inverse).astype(BF16)
-
-    def stacked(h):
-        return jnp.concatenate([up(h, g) for g in range(8)], axis=0)
-
-    zero = jnp.zeros((16, HD), BF16)
-    queries = jnp.concatenate([stacked(0), stacked(1)], axis=1)
-
-    def near(first, second):
-        return jnp.concatenate(
-            [jnp.concatenate([first, zero], axis=1), jnp.concatenate([zero, second], axis=1)],
-            axis=0,
-        )
-
-    near_keys = near(up(0, 8), up(1, 8))
-    near_values = near(up(0, 9), up(1, 9))
-    far = contract(queries, head_halves(k_ref[...]), ((1,), (1,))) * SCALE2
-    far = far + jnp.where(usable > 0.5, 0.0, MASKED)
+    def up(b):
+        return (raw[16 * b : 16 * b + 16] * inverse).astype(BF16)
+
+    queries = jnp.concatenate([up(g) for g in range(8)], axis=0)
+    near_keys, near_values = up(8), up(9)
+    count = (mine_ref.shape[0] - 16) // 2
+    parts = []
+    for ref in (mine_ref, other_ref):
+        limits = ref[2 * count : 2 * count + 16, :].astype(F32)
+        part = contract(queries, ref[0:count, :], ((1,), (1,))) * SCALE2
+        for c in range(0, count, HD):
+            usable = limits[c // HD : c // HD + 1] > 0.5
+            parts.append(jnp.where(usable, part[:, c : c + HD], MASKED))
     row_pick = (
-        lax.broadcasted_iota(jnp.int32, (128, 16), 0) % 16
-        == lax.broadcasted_iota(jnp.int32, (128, 16), 1)
-    )
-    col_pick = (
-        lax.broadcasted_iota(jnp.int32, (16, 32), 1) % 16
-        == lax.broadcasted_iota(jnp.int32, (16, 32), 0)
+        lax.broadcasted_iota(jnp.int32, (HD, 16), 0) % 16
+        == lax.broadcasted_iota(jnp.int32, (HD, 16), 1)
     )
     ancestry = anc_ref[request].astype(F32).astype(BF16)
-    seen = contract(ancestry, col_pick.astype(F32).astype(BF16), ((1,), (0,)))
-    seen = contract(row_pick.astype(F32).astype(BF16), seen.astype(BF16), ((1,), (0,)))
+    seen = contract(row_pick.astype(F32).astype(BF16), ancestry, ((1,), (0,)))
     close = contract(queries, near_keys, ((1,), (1,))) * SCALE2
     close = jnp.where((seen > 0.5) & leader, close, MASKED)
-    second = lax.broadcasted_iota(jnp.int32, close.shape, 1) >= 16
-    n0 = jnp.max(jnp.where(second, MASKED, close), axis=1, keepdims=True)
-    n1 = jnp.max(jnp.where(second, close, MASKED), axis=1, keepdims=True)
-    m0, m1, odd = pair_max(far)
-    s0, s1 = shift_of(jnp.maximum(m0, n0)), shift_of(jnp.maximum(m1, n1))
-    weights, l0, l1 = pair_weights(far, s0, s1, odd)
-    close_w = jnp.exp2(close - jnp.where(second, s1, s0))
-    l0 = l0 + jnp.sum(jnp.where(second, 0.0, close_w), axis=1, keepdims=True)
-    l1 = l1 + jnp.sum(jnp.where(second, close_w, 0.0), axis=1, keepdims=True)
-    blend = contract(weights, head_halves(v_ref[...]), ((1,), (0,)))
-    blend = blend + contract(close_w.astype(BF16), near_values, ((1,), (0,)))
-    lane = lax.broadcasted_iota(jnp.int32, (128, HD), 1)
-    stats = [jnp.where(lane < 64, s0, l0), jnp.where(lane < 64, s1, l1)]
-    for h in range(2):
-        for g in range(8):
-            for half in range(2):
-                at = 16 * g + 8 * half
-                to = pl.ds(8 * half * 16 + 8 * h + g, 8, stride=16)
-                blend_scr[to, :] = blend[at : at + 8, h * HD : (h + 1) * HD]
-                stat_scr[to, :] = stats[h][at : at + 8]
-    lane = lax.broadcasted_iota(jnp.int32, (16, HD), 1)
+    folded = parts[0]
+    for part in parts[1:]:
+        folded = jnp.maximum(folded, part)
+    top = jnp.maximum(
+        jnp.max(folded, axis=1, keepdims=True), jnp.max(close, axis=1, keepdims=True)
+    )
+    shift = shift_of(top)
+    weights = [jnp.exp2(part - shift) for part in parts]
+    near_w = jnp.exp2(close - shift)
+    total = weights[0]
+    for w in weights[1:]:
+        total = total + w
+    sums = jnp.sum(total, axis=1, keepdims=True) + jnp.sum(near_w, axis=1, keepdims=True)
+    blend = contract(near_w.astype(BF16), near_values, ((1,), (0,)))
+    half = len(parts) // 2
+    for n, ref in enumerate((mine_ref, other_ref)):
+        group = [w.astype(BF16) for w in weights[n * half : (n + 1) * half]]
+        blend = blend + contract(
+            jnp.concatenate(group, axis=1), ref[count : 2 * count, :], ((1,), (0,))
+        )
+    lane = lax.broadcasted_iota(jnp.int32, (HD, HD), 1)
+    stats = jnp.where(lane < 64, shift, sums)
+    for g in range(8):
+        for node in (0, 8):
+            at = 16 * g + node
+            to = pl.ds(8 * node + g, 8, stride=8)
+            blend_scr[to, :] = blend[at : at + 8]
+            stat_scr[to, :] = stats[at : at + 8]
     for j in range(GROUP):
-        out_ref[j, 0:32, :] = blend_scr[32 * j : 32 * j + 32, :].astype(BF16)
-        out_ref[j, 32:48, :] = jnp.where(
-            lane % 2 == 0, stat_scr[32 * j : 32 * j + 16, :], stat_scr[32 * j + 16 : 32 * j + 32, :]
-        ).astype(BF16)
-
-
-def retained_attend(width, lengths, gathered, keys, values, positions, ancestors):
+        out_ref[j, 0:16, :] = blend_scr[16 * j : 16 * j + 16, :].astype(BF16)
+        out_ref[j, 16:32, :] = stat_scr[16 * j : 16 * j + 16, :].astype(BF16)
+
+
+def retained_attend(width, summed, mine, other, ancestors):
     vmem = pl.BlockSpec(memory_space=pltpu.VMEM)
     return pl.pallas_call(
         functools.partial(retained_kernel, width),
-        in_specs=[pl.BlockSpec(memory_space=pltpu.SMEM), vmem, vmem, vmem, vmem, vmem],
+        in_specs=[vmem, vmem, vmem, vmem],
         out_specs=vmem,
-        out_shape=jax.ShapeDtypeStruct((GROUP, 48, HD), BF16),
-        scratch_shapes=[pltpu.VMEM((256, HD), F32), pltpu.VMEM((256, HD), F32)],
+        out_shape=jax.ShapeDtypeStruct((GROUP, 32, HD), BF16),
+        scratch_shapes=[pltpu.VMEM((HD, HD), F32), pltpu.VMEM((HD, HD), F32)],
         compiler_params=pltpu.CompilerParams(vmem_limit_bytes=8 << 20),
         name="retained_attend",
-    )(lengths, gathered, keys, values, positions, ancestors)
+    )(summed, mine, other, ancestors)
 
 
 def finish_kernel(parts_ref, out_ref):
-    stats = parts_ref[:, 32:48, :].astype(F32)
-    highest = jnp.max(stats, axis=0)
-    factor = jnp.exp2(jnp.minimum(stats - highest[None], 0.0))
-    sums = pltpu.roll(stats.reshape(-1, HD), 64, 1).reshape(stats.shape)
-    total = jnp.sum(sums * factor, axis=0)
-    for i in range(2):
-        rows = parts_ref[:, 16 * i : 16 * i + 16, :].astype(F32)
-        blend = jnp.sum(rows * factor[:, :, i : i + 1], axis=0)
-        heads = blend / total[:, i : i + 1]
-        for c in range(16):
-            out_ref[i : i + 1, c * HD : (c + 1) * HD] = heads[c : c + 1]
+    for h in range(2):
+        sources = [2 * z + h for z in range(4)]
+        stats = [parts_ref[a, 16:32, :].astype(F32) for a in sources]
+        highest = stats[0]
+        for stat in stats[1:]:
+            highest = jnp.maximum(highest, stat)
+        blend = None
+        total = None
+        for a, stat in zip(sources, stats):
+            factor = jnp.exp2(stat[:, 0:1] - highest[:, 0:1])
+            part = parts_ref[a, 0:16, :].astype(F32) * factor
+            weight = stat[:, 64:65] * factor
+            blend = part if blend is None else blend + part
+            total = weight if total is None else total + weight
+        heads = blend / total
+        for i in range(2):
+            for g in range(8):
+                at = 8 * h + g
+                out_ref[i : i + 1, at * HD : (at + 1) * HD] = heads[8 * i + g : 8 * i + g + 1]
 
 
 def finish_upper(parts):
@@ -534,7 +526,7 @@
         finish_kernel,
         out_shape=jax.ShapeDtypeStruct((2, 16 * HD), F32),
         name="finish_upper",
-    )(parts)
+    )(pltpu.with_memory_space_constraint(parts, pltpu.VMEM))
 
 
 def swapped(array, axis):
@@ -571,6 +563,13 @@
         ],
         axis=0,
     )
+    kept_own, kept_given = split_heads(
+        cache_lengths,
+        retained_keys.reshape(kept * kv_heads, HD),
+        retained_values.reshape(kept * kv_heads, HD),
+        retained_index[0].T,
+    )
+    kept_other = swapped(kept_given, "yh")
     queries = spread(spread(own_q, DEPTH).reshape(-1, HD), FACE).reshape(GROUP, GROUP, 32, HD)
     turned_keys = turn(cache_keys.reshape(requests, cache_part * kv_heads, HD))
     parts = cache_attend(
@@ -589,17 +588,10 @@
         tree_hidden, terms, norm_gain.reshape(1, -1), w_query_up, w_key_up, w_value_up
     )
     summed = jnp.sum(exchanged(projected, FACE).astype(F32), axis=0).astype(BF16)
-    shares = jnp.broadcast_to(summed.reshape(2, 1, 176, HD), (2, GROUP, 176, HD))
-    gathered = exchanged(shares.reshape(2 * GROUP, 176, HD), SIDE)
-    upper = retained_attend(
-        width,
-        cache_lengths,
-        gathered,
-        retained_keys.reshape(kept * kv_heads, HD),
-        retained_values.reshape(kept * kv_heads, HD),
-        retained_index[0].T,
-        ancestors,
-    )
+    shares = jnp.broadcast_to(summed.reshape(2, 1, 176, HD), (2, 4, 176, HD))
+    arrived = exchanged(shares.reshape(GROUP, 176, HD), DEPTH)
+    mine = jnp.sum(arrived.astype(F32), axis=0).astype(BF16)
+    upper = retained_attend(width, mine, kept_own, kept_other, ancestors)
     upper_heads = finish_upper(exchanged(upper, TEAM))
     return (residual, upper_heads)
 

time: 150 us -> 140 us (0.933)
  blocking collectives: 113 us -> 88 us
  waiting for transfers between devices: 9.24 us -> 19.7 us
  starting transfers between devices: 7.56 us -> 12.2 us
    all_to_all x7 -> x6, blocking collectives: 113 us -> 88 us  [exchanged(): return lax.all_to_all(blocks, axis, split_axis=0, concat_axis=0, tiled=True)]
    all_to_all x1 -> x2, waiting for transfers between devices: 5.08 us -> 15.5 us  [exchanged(): return lax.all_to_all(blocks, axis, split_axis=0, concat_axis=0, tiled=True)]
    all_to_all x1 -> x2, starting transfers between devices: 6.03 us -> 9.47 us  [exchanged(): return lax.all_to_all(blocks, axis, split_axis=0, concat_axis=0, tiled=True)]
    unnamed x29 -> x27, local copies, waits for them, and re-layouts: 2.74 us -> 0.77 us
    ppermute x2 -> x3, waiting for transfers between devices: 4.16 us -> 4.16 us  [swapped(): return lax.ppermute(array, axis, [(0, 1), (1, 0)])]
  transfers between devices with their start and end apart: 3 -> 5, of which waited for: 3 -> 4; matrix products, arithmetic and copies ran while one was open for 0% -> 0% of each run, Pallas kernels for 2% -> 3%
where the time goes in v3:
time: 140 us; the launch traced here: 139 us
  blocking collectives  88 us (63%)
  waiting for transfers between devices  19.7 us (14%)
  Pallas kernels  15.8 us (11%)
  starting transfers between devices  12.2 us (9%)
  local copies, waits for them, and re-layouts  2.57 us (2%)
    all_to_all x6, blocking collectives, exchanged(): return lax.all_to_all(blocks, axis, split_axis=0, concat_axis=0, tiled=True)  88 us
    all_to_all x2, waiting for transfers between devices, exchanged(): return lax.all_to_all(blocks, axis, split_axis=0, concat_axis=0, tiled=True)  15.5 us
    all_to_all x2, starting transfers between devices, exchanged(): return lax.all_to_all(blocks, axis, split_axis=0, concat_axis=0, tiled=True)  9.47 us
    pallas_call x1, Pallas kernels, cache_attend(): pl.pallas_call(cache_kernel, in_specs=[pl.BlockSpec(memory_space=pltpu.SM...  7.08 us
    ppermute x3, waiting for transfers between devices, swapped(): return lax.ppermute(array, axis, [(0, 1), (1, 0)])  4.16 us
    pallas_call x1, Pallas kernels, turn(): pl.pallas_call(turn_kernel, in_specs=[pl.BlockSpec(memory_space=pltpu.HBM...  3.55 us
  transfers between devices with their start and end apart: 5, of which 4 were waited for; matrix products, arithmetic and copies ran while one was open for 0% of the time, Pallas kernels for 3%

profile of v3, /device:TPU:8, one launch (start us, length us, event | category | flops | bytes accessed | tf_op | source)
XLA Modules:
  0.0 139.4 jit_solution(4000622535696902)
XLA Ops:
  0.6 0.7 copy.30
  1.4 16.6 %all_to_all.40 = bf16[8,32,128]{2,1,0:T(8,128)(2,1)S(1)} all-to-all(bf16[8,32,128]{2,1,0:T(8,128)(2,1)S(1)} %broadcast_in_dim.19), channel_id=1, replica_groups=mesh['x'=4,'zh'=2,'zl'=4,'yh'=2,'yl'=2,'c'=2] {'zh','zl'}, dimensions={0} | all-to-all | bytes 131072 | tf_op jit(solution)/shard_map/all_to_all | solution.py:31
  18.0 0.9 broadcast_in_dim.20
  18.9 6.0 %all-to-all-start.1 = ((bf16[8,256,128]{2,1,0:T(8,128)(2,1)}), bf16[8,256,128]{2,1,0:T(8,128)(2,1)S(1)}, u32[]{:S(2)}, u32[]{:S(2)}) async-start(bf16[8,256,128]{2,1,0:T(8,128)(2,1)} %broadcast_in_dim.20), calls=%async_computation.1 | async-start | bytes 1048576 | tf_op jit(solution)/shard_map/all_to_all | solution.py:31
  24.9 3.5 %turn.1.kt_hbm = bf16[8,128,2048]{2,1,0:T(8,128)(2,1)} custom-call(bf16[8,2048,128]{2,1,0:T(8,128)(2,1)} %bitcast.37), custom_call_target="tpu_custom_call" | custom-call | tf_op jit(solution)/shard_map/turn/pallas_call | solution.py:77
  28.5 6.1 %all-to-all-done.1 = bf16[8,256,128]{2,1,0:T(8,128)(2,1)S(1)} async-done(((bf16[8,256,128]{2,1,0:T(8,128)(2,1)}), bf16[8,256,128]{2,1,0:T(8,128)(2,1)S(1)}, u32[]{:S(2)}, u32[]{:S(2)}) %all-to-all-start.1) | async-done | bytes 524320 | tf_op jit(solution)/shard_map/all_to_all | solution.py:31
  34.7 7.1 %cache_attend.1 = bf16[8,272,128]{2,1,0:T(8,128)(2,1)S(1)} custom-call(s32[8]{0:T(128)S(1)} %copy-done.9, bf16[8,8,32,128]{3,2,1,0:T(8,128)(2,1)S(1)} %bitcast.31, bf16[8,128,2048]{2,1,0:T(8,128)(2,1)} %turn.1.kt_hbm, bf16[8,2048,128]{2,1,0:T(8,128)(2,1)} %bitcast.38, bf16[8,128]{1,0:T(8,128)(2,1)S(1)} %pad_maximum_fusion.kv_ref), custom_call_target="tpu_custom_call" | custom-call | tf_op jit(solution)/shard_map/cache_attend/pallas_call | solution.py:196
  41.8 13.6 %all_to_all.41.parts_ref = bf16[8,272,128]{2,1,0:T(8,128)(2,1)S(1)} all-to-all(bf16[8,272,128]{2,1,0:T(8,128)(2,1)S(1)} %cache_attend.1), channel_id=1, replica_groups=mesh['x'=4,'zh'=2,'zl'=4,'yh'=2,'yl'=2,'c'=2] {'x','yh'}, dimensions={0} | all-to-all | bytes 1114112 | tf_op jit(solution)/shard_map/all_to_all | solution.py:31
  56.0 18.4 %all_to_all.42.parts_ref = bf16[8,272,128]{2,1,0:T(8,128)(2,1)S(1)} all-to-all(bf16[8,272,128]{2,1,0:T(8,128)(2,1)S(1)} %broadcast_in_dim.21), channel_id=1, replica_groups=mesh['x'=4,'zh'=2,'zl'=4,'yh'=2,'yl'=2,'c'=2] {'zh','zl'}, dimensions={0} | all-to-all | bytes 1114112 | tf_op jit(solution)/shard_map/all_to_all | solution.py:31
  74.5 1.3 merge_lower.1
  75.8 12.6 %all_to_all.43.heads_ref = bf16[8,32,1024]{2,1,0:T(8,128)(2,1)S(1)} all-to-all(bf16[8,32,1024]{2,1,0:T(8,128)(2,1)S(1)} %broadcast_in_dim.22), channel_id=1, replica_groups=mesh['x'=4,'zh'=2,'zl'=4,'yh'=2,'yl'=2,'c'=2] {'x','yh'}, dimensions={0} | all-to-all | bytes 1048576 | tf_op jit(solution)/shard_map/all_to_all | solution.py:31
  88.8 1.2 collective-permute-done
  90.1 1.4 %collective-permute-start.1 = (f32[128,128]{1,0:T(8,128)S(1)}, f32[128,128]{1,0:T(8,128)S(1)}, u32[]{:S(2)}, u32[]{:S(2)}) collective-permute-start(f32[128,128]{1,0:T(8,128)S(1)} %add.6), channel_id=1, source_target_pairs={{0,2},{2,0},{1,3},{3,1},{4,6},{6,4},{5,7},{7,5},{8,10},{10,8},{9,1... | collective-permute-start | bytes 196616 | tf_op jit(solution)/shard_map/ppermute | solution.py:533
  91.5 2.9 %collective-permute-done.1 = f32[128,128]{1,0:T(8,128)S(1)} collective-permute-done((f32[128,128]{1,0:T(8,128)S(1)}, f32[128,128]{1,0:T(8,128)S(1)}, u32[]{:S(2)}, u32[]{:S(2)}) %collective-permute-start.1) | collective-permute-done | bytes 65568 | tf_op jit(solution)/shard_map/ppermute | solution.py:533
  94.5 0.7 project.1
  95.2 15.5 %all_to_all.44 = bf16[8,352,128]{2,1,0:T(8,128)(2,1)S(1)} all-to-all(bf16[8,352,128]{2,1,0:T(8,128)(2,1)S(1)} %get-tuple-element.7), channel_id=1, replica_groups=mesh['x'=4,'zh'=2,'zl'=4,'yh'=2,'yl'=2,'c'=2] {'x','yh'}, dimensions={0} | all-to-all | bytes 1441792 | tf_op jit(solution)/shard_map/all_to_all | solution.py:31
  110.8 0.8 broadcast_in_dim.24
  111.5 3.4 %all-to-all-start.6 = ((bf16[8,176,128]{2,1,0:T(8,128)(2,1)}), bf16[8,176,128]{2,1,0:T(8,128)(2,1)S(1)}, u32[]{:S(2)}, u32[]{:S(2)}) async-start(bf16[8,176,128]{2,1,0:T(8,128)(2,1)} %bitcast.14), calls=%async_computation.6 | async-start | bytes 720896 | tf_op jit(solution)/shard_map/all_to_all | solution.py:31
  115.0 1.0 split_heads.1
  116.0 1.2 collective-permute-start.2
  117.2 9.4 %all-to-all-done.6 = bf16[8,176,128]{2,1,0:T(8,128)(2,1)S(1)} async-done(((bf16[8,176,128]{2,1,0:T(8,128)(2,1)}), bf16[8,176,128]{2,1,0:T(8,128)(2,1)S(1)}, u32[]{:S(2)}, u32[]{:S(2)}) %all-to-all-start.6) | async-done | bytes 360480 | tf_op jit(solution)/shard_map/all_to_all | solution.py:31
  126.7 0.7 retained_attend.1
  127.4 11.2 %all_to_all.45.parts_ref = bf16[8,32,128]{2,1,0:T(8,128)(2,1)S(1)} all-to-all(bf16[8,32,128]{2,1,0:T(8,128)(2,1)S(1)} %retained_attend.1), channel_id=1, replica_groups=mesh['x'=4,'zh'=2,'zl'=4,'yh'=2,'yl'=2,'c'=2] {'zl','yh'}, dimensions={0} | all-to-all | bytes 131072 | tf_op jit(solution)/shard_map/all_to_all | solution.py:31
  138.6 0.8 finish_upper.1
  (39 shorter events, 1.3 us)
Async XLA Ops:
  18.9 15.8 %all-to-all-start.1 = ((bf16[8,256,128]{2,1,0:T(8,128)(2,1)}), bf16[8,256,128]{2,1,0:T(8,128)(2,1)S(1)}, u32[]{:S(2)}, u32[]{:S(2)}) async-start(bf16[8,256,128]{2,1,0:T(8,128)(2,1)} %broadcast_in_dim.20), calls=%async_computation.1 | async-start | bytes 1048576 | tf_op jit(solution)/shard_map/all_to_all | solution.py:31
  24.9 3.6 %copy-start.11 = (bf16[2,256]{1,0:T(2,128)(2,1)S(1)}, bf16[2,256]{1,0:T(2,128)(2,1)}, u32[]{:S(2)}) copy-start(bf16[2,256]{1,0:T(2,128)(2,1)} %param.19) | copy-start | bytes 3076
  24.9 3.6 %copy-start.12 = (bf16[2,256]{1,0:T(2,128)(2,1)S(1)}, bf16[2,256]{1,0:T(2,128)(2,1)}, u32[]{:S(2)}) copy-start(bf16[2,256]{1,0:T(2,128)(2,1)} %param.18) | copy-start | bytes 3076
  24.9 9.7 %copy-start.9 = (s32[8]{0:T(128)S(1)}, s32[8]{0:T(128)}, u32[]{:S(2)}) copy-start(s32[8]{0:T(128)} %len_ref.3) | copy-start | bytes 100
  34.7 39.8 %copy-start.4 = (s32[8,16,16]{2,1,0:T(8,128)S(1)}, s32[8,16,16]{2,1,0:T(8,128)}, u32[]{:S(2)}) copy-start(s32[8,16,16]{2,1,0:T(8,128)} %anc_ref.3) | copy-start | bytes 24580
  41.7 46.7 %copy-start.1 = (bf16[2048,128]{1,0:T(8,128)(2,1)S(1)}, bf16[2048,128]{1,0:T(8,128)(2,1)}, u32[]{:S(2)}) copy-start(bf16[2048,128]{1,0:T(8,128)(2,1)} %weight_ref.1) | copy-start | bytes 1572868
  41.8 52.7 %copy-start = (bf16[128,2048]{1,0:T(8,128)(2,1)S(1)}, bf16[128,2048]{1,0:T(8,128)(2,1)}, u32[]{:S(2)}) copy-start(bf16[128,2048]{1,0:T(8,128)(2,1)} %wq_ref.1) | copy-start | bytes 1572868
  41.8 52.7 %copy-start.5 = (bf16[128,256]{1,0:T(8,128)(2,1)S(1)}, bf16[128,256]{1,0:T(8,128)(2,1)}, u32[]{:S(2)}) copy-start(bf16[128,256]{1,0:T(8,128)(2,1)} %wk_ref.1) | copy-start | bytes 196612
  41.8 52.7 %copy-start.6 = (bf16[128,256]{1,0:T(8,128)(2,1)S(1)}, bf16[128,256]{1,0:T(8,128)(2,1)}, u32[]{:S(2)}) copy-start(bf16[128,256]{1,0:T(8,128)(2,1)} %wv_ref.1) | copy-start | bytes 196612
  41.8 52.7 %copy-start.7 = (bf16[128,128]{1,0:T(8,128)(2,1)S(1)}, bf16[128,128]{1,0:T(8,128)(2,1)}, u32[]{:S(2)}) copy-start(bf16[128,128]{1,0:T(8,128)(2,1)} %hidden_ref.1) | copy-start | bytes 98308
  41.8 52.7 %copy-start.10 = (f32[128]{0:T(128)S(1)}, f32[128]{0:T(128)}, u32[]{:S(2)}) copy-start(f32[128]{0:T(128)} %param.25) | copy-start | bytes 1540
  74.5 40.5 %copy-start.2 = (bf16[1,512,2,128]{3,2,1,0:T(2,128)(2,1)S(1)}, bf16[1,512,2,128]{3,2,1,0:T(2,128)(2,1)}, u32[]{:S(2)}) copy-start(bf16[1,512,2,128]{3,2,1,0:T(2,128)(2,1)} %param.29) | copy-start | bytes 786436
  74.5 40.5 %copy-start.3 = (bf16[1,512,2,128]{3,2,1,0:T(2,128)(2,1)S(1)}, bf16[1,512,2,128]{3,2,1,0:T(2,128)(2,1)}, u32[]{:S(2)}) copy-start(bf16[1,512,2,128]{3,2,1,0:T(2,128)(2,1)} %param.30) | copy-start | bytes 786436
  74.5 40.6 %copy-start.8 = (s32[1,512,2]{1,2,0:T(2,128)S(1)}, s32[1,512,2]{1,2,0:T(2,128)}, u32[]{:S(2)}) copy-start(s32[1,512,2]{1,2,0:T(2,128)} %param.31) | copy-start | bytes 12292
  88.7 1.3 collective-permute-start
  90.1 4.4 %collective-permute-start.1 = (f32[128,128]{1,0:T(8,128)S(1)}, f32[128,128]{1,0:T(8,128)S(1)}, u32[]{:S(2)}, u32[]{:S(2)}) collective-permute-start(f32[128,128]{1,0:T(8,128)S(1)} %add.6), channel_id=1, source_target_pairs={{0,2},{2,0},{1,3},{3,1},{4,6},{6,4},{5,7},{7,5},{8,10},{10,8},{9,1... | collective-permute-start | bytes 196616 | tf_op jit(solution)/shard_map/ppermute | solution.py:533
  111.5 15.1 %all-to-all-start.6 = ((bf16[8,176,128]{2,1,0:T(8,128)(2,1)}), bf16[8,176,128]{2,1,0:T(8,128)(2,1)S(1)}, u32[]{:S(2)}, u32[]{:S(2)}) async-start(bf16[8,176,128]{2,1,0:T(8,128)(2,1)} %bitcast.14), calls=%async_computation.6 | async-start | bytes 720896 | tf_op jit(solution)/shard_map/all_to_all | solution.py:31
  116.0 10.7 %collective-permute-start.2 = (bf16[1040,128]{1,0:T(8,128)(2,1)S(1)}, bf16[1040,128]{1,0:T(8,128)(2,1)S(1)}, u32[]{:S(2)}, u32[]{:S(2)}) collective-permute-start(bf16[1040,128]{1,0:T(8,128)(2,1)S(1)} %get-tuple-element.9), channel_id=1, source_target_pairs={{0,4},{4,0},{1,5},{5,1},{2,6},{6,2},{3,7},{7,3},{8,12},{12,8},{9,1... | collective-permute-start | bytes 798728 | tf_op jit(solution)/shard_map/ppermute | solution.py:533

commit v4 on v3

--- a/solution.py
+++ b/solution.py
@@ -17,9 +17,9 @@
 F32 = jnp.float32
 BF16 = jnp.bfloat16
 
-SEQ = ("x", "zh", "zl", "yh")
-TEAM = ("zl", "yh")
-DEPTH = ("zh", "zl")
+SEQ = ("x", "zh", "z1", "z0", "yh")
+TEAM = ("z1", "yh")
+DEPTH = ("zh", "z1", "z0")
 FACE = ("x", "yh")
 
 
@@ -31,8 +31,10 @@
     return lax.all_to_all(blocks, axis, split_axis=0, concat_axis=0, tiled=True)
 
 
-def spread(array, axis):
+def spread(array, axis, near=False):
     copies = jnp.broadcast_to(array, (lax.axis_size(axis), *array.shape))
+    if near:
+        copies = pltpu.with_memory_space_constraint(copies, pltpu.VMEM)
     return exchanged(copies, axis)
 
 
@@ -425,10 +427,13 @@
     )(lengths, keys, values, positions)
 
 
-def retained_kernel(width, sum_ref, mine_ref, other_ref, anc_ref, out_ref, blend_scr, stat_scr):
+def retained_kernel(width, terms_ref, a_ref, b_ref, c_ref, d_ref, anc_ref, out_ref, blend_scr, stat_scr):
+    kept_refs = (a_ref, b_ref, c_ref, d_ref)
     request = lax.axis_index(SEQ) // GROUP
-    leader = lax.axis_index("zl") == 0
-    raw = sum_ref[...].astype(F32)
+    leader = lax.axis_index("z1") == 0
+    raw = terms_ref[0].astype(F32)
+    for z in range(1, GROUP):
+        raw = raw + terms_ref[z].astype(F32)
     square = raw[160:176, 0:1] + raw[160:176, 64:65]
     inverse = lax.rsqrt(square / width + EPS)
 
@@ -437,9 +442,9 @@
 
     queries = jnp.concatenate([up(g) for g in range(8)], axis=0)
     near_keys, near_values = up(8), up(9)
-    count = (mine_ref.shape[0] - 16) // 2
+    count = (a_ref.shape[0] - 16) // 2
     parts = []
-    for ref in (mine_ref, other_ref):
+    for ref in kept_refs:
         limits = ref[2 * count : 2 * count + 16, :].astype(F32)
         part = contract(queries, ref[0:count, :], ((1,), (1,))) * SCALE2
         for c in range(0, count, HD):
@@ -467,9 +472,9 @@
         total = total + w
     sums = jnp.sum(total, axis=1, keepdims=True) + jnp.sum(near_w, axis=1, keepdims=True)
     blend = contract(near_w.astype(BF16), near_values, ((1,), (0,)))
-    half = len(parts) // 2
-    for n, ref in enumerate((mine_ref, other_ref)):
-        group = [w.astype(BF16) for w in weights[n * half : (n + 1) * half]]
+    share = len(parts) // len(kept_refs)
+    for n, ref in enumerate(kept_refs):
+        group = [w.astype(BF16) for w in weights[n * share : (n + 1) * share]]
         blend = blend + contract(
             jnp.concatenate(group, axis=1), ref[count : 2 * count, :], ((1,), (0,))
         )
@@ -481,27 +486,29 @@
             to = pl.ds(8 * node + g, 8, stride=8)
             blend_scr[to, :] = blend[at : at + 8]
             stat_scr[to, :] = stats[at : at + 8]
-    for j in range(GROUP):
-        out_ref[j, 0:16, :] = blend_scr[16 * j : 16 * j + 16, :].astype(BF16)
-        out_ref[j, 16:32, :] = stat_scr[16 * j : 16 * j + 16, :].astype(BF16)
-
-
-def retained_attend(width, summed, mine, other, ancestors):
+    for j in range(4):
+        member = (j // 2) * 4 + lax.axis_index("z0") * 2 + j % 2
+        rows = pl.ds(pl.multiple_of(16 * member, 16), 16)
+        out_ref[j, 0:16, :] = blend_scr[rows, :].astype(BF16)
+        out_ref[j, 16:32, :] = stat_scr[rows, :].astype(BF16)
+
+
+def retained_attend(width, terms, kept, ancestors):
     vmem = pl.BlockSpec(memory_space=pltpu.VMEM)
     return pl.pallas_call(
         functools.partial(retained_kernel, width),
-        in_specs=[vmem, vmem, vmem, vmem],
+        in_specs=[vmem] * (2 + len(kept)),
         out_specs=vmem,
-        out_shape=jax.ShapeDtypeStruct((GROUP, 32, HD), BF16),
+        out_shape=jax.ShapeDtypeStruct((4, 32, HD), BF16),
         scratch_shapes=[pltpu.VMEM((HD, HD), F32), pltpu.VMEM((HD, HD), F32)],
         compiler_params=pltpu.CompilerParams(vmem_limit_bytes=8 << 20),
         name="retained_attend",
-    )(summed, mine, other, ancestors)
+    )(terms, *kept, ancestors)
 
 
 def finish_kernel(parts_ref, out_ref):
     for h in range(2):
-        sources = [2 * z + h for z in range(4)]
+        sources = [2 * z + h for z in range(2)]
         stats = [parts_ref[a, 16:32, :].astype(F32) for a in sources]
         highest = stats[0]
         for stat in stats[1:]:
@@ -530,7 +537,8 @@
 
 
 def swapped(array, axis):
-    return lax.ppermute(array, axis, [(0, 1), (1, 0)])
+    last = lax.axis_size(axis) - 1
+    return lax.ppermute(array, axis, [(i, last - i) for i in range(last + 1)])
 
 
 def shards(
@@ -569,8 +577,7 @@
         retained_values.reshape(kept * kv_heads, HD),
         retained_index[0].T,
     )
-    kept_other = swapped(kept_given, "yh")
-    queries = spread(spread(own_q, DEPTH).reshape(-1, HD), FACE).reshape(GROUP, GROUP, 32, HD)
+    queries = spread(spread(own_q, DEPTH), FACE, True)
     turned_keys = turn(cache_keys.reshape(requests, cache_part * kv_heads, HD))
     parts = cache_attend(
         cache_lengths,
@@ -588,17 +595,24 @@
         tree_hidden, terms, norm_gain.reshape(1, -1), w_query_up, w_key_up, w_value_up
     )
     summed = jnp.sum(exchanged(projected, FACE).astype(F32), axis=0).astype(BF16)
+    held = (
+        kept_own,
+        swapped(kept_given, "yh"),
+        swapped(kept_own, "z0"),
+        swapped(kept_given, ("z0", "yh")),
+    )
+    summed, held = lax.optimization_barrier((summed, held))
     shares = jnp.broadcast_to(summed.reshape(2, 1, 176, HD), (2, 4, 176, HD))
     arrived = exchanged(shares.reshape(GROUP, 176, HD), DEPTH)
-    mine = jnp.sum(arrived.astype(F32), axis=0).astype(BF16)
-    upper = retained_attend(width, mine, kept_own, kept_other, ancestors)
+    upper = retained_attend(width, arrived, held, ancestors)
     upper_heads = finish_upper(exchanged(upper, TEAM))
     return (residual, upper_heads)
 
 
 def solution(mesh):
     fine = Mesh(
-        mesh.devices.reshape(4, 2, 4, 2, 2, 2), ("x", "zh", "zl", "yh", "yl", "c")
+        mesh.devices.reshape(4, 2, 2, 2, 2, 2, 2),
+        ("x", "zh", "z1", "z0", "yh", "yl", "c"),
     )
     seq, tp = SEQ, ("yl", "c")
     return jax.shard_map(

time: 140 us -> 151 us (1.079); the launches traced: 139 us -> 149 us
  waiting for transfers between devices: 19.7 us -> 26.5 us
  starting transfers between devices: 12.2 us -> 16.2 us
    ppermute x3 -> x5, starting transfers between devices: 2.74 us -> 6.61 us  [swapped(): return lax.ppermute(array, axis, [(i, last - i) for i in range(last + 1)])]
    ppermute x3 -> x5, waiting for transfers between devices: 4.16 us -> 7.83 us  [swapped(): return lax.ppermute(array, axis, [(i, last - i) for i in range(last + 1)])]
    all_to_all x2, waiting for transfers between devices: 15.5 us -> 18.7 us  [exchanged(): return lax.all_to_all(blocks, axis, split_axis=0, concat_axis=0, tiled=True)]
  transfers between devices with their start and end apart: 5 -> 7, of which waited for: 4 -> 5; matrix products, arithmetic and copies ran while one was open for 0% -> 0% of each run, Pallas kernels for 3% -> 3%
where the time goes in v4:
time: 151 us; the launch traced here: 149 us
  blocking collectives  86.6 us (57%)
  waiting for transfers between devices  26.5 us (18%)
  Pallas kernels  16.5 us (11%)
  starting transfers between devices  16.2 us (11%)
  local copies, waits for them, and re-layouts  1.85 us (1%)
    all_to_all x6, blocking collectives, exchanged(): return lax.all_to_all(blocks, axis, split_axis=0, concat_axis=0, tiled=True)  86.6 us
    all_to_all x2, waiting for transfers between devices, exchanged(): return lax.all_to_all(blocks, axis, split_axis=0, concat_axis=0, tiled=True)  18.7 us
    all_to_all x2, starting transfers between devices, exchanged(): return lax.all_to_all(blocks, axis, split_axis=0, concat_axis=0, tiled=True)  9.57 us
    ppermute x5, waiting for transfers between devices, swapped(): return lax.ppermute(array, axis, [(i, last - i) for i in range(last + 1)])  7.83 us
    pallas_call x1, Pallas kernels, cache_attend(): pl.pallas_call(cache_kernel, in_specs=[pl.BlockSpec(memory_space=pltpu.SM...  7.07 us
    ppermute x5, starting transfers between devices, swapped(): return lax.ppermute(array, axis, [(i, last - i) for i in range(last + 1)])  6.61 us
    pallas_call x1, Pallas kernels, turn(): pl.pallas_call(turn_kernel, in_specs=[pl.BlockSpec(memory_space=pltpu.HBM...  3.51 us
  transfers between devices with their start and end apart: 7, of which 5 were waited for; matrix products, arithmetic and copies ran while one was open for 0% of the time, Pallas kernels for 3%

profile of v4, /device:TPU:8, one launch (start us, length us, event | category | flops | bytes accessed | tf_op | source)
XLA Modules:
  0.0 148.7 jit_solution(9809188342519841156)
XLA Ops:
  1.4 16.6 %all_to_all.40 = bf16[8,32,128]{2,1,0:T(8,128)(2,1)S(1)} all-to-all(bf16[8,32,128]{2,1,0:T(8,128)(2,1)S(1)} %broadcast_in_dim.19), channel_id=1, replica_groups=mesh['x'=4,'zh'=2,'z1'=2,'z0'=2,'yh'=2,'yl'=2,'c'=2] {'zh','z1','z0'}, dimensions={0} | all-to-all | bytes 131072 | tf_op jit(solution)/shard_map/all_to_all | solution.py:31
  18.0 0.9 broadcast_in_dim.20
  18.9 6.0 %all-to-all-start.1 = ((bf16[8,8,32,128]{3,2,1,0:T(8,128)(2,1)}), bf16[8,8,32,128]{3,2,1,0:T(8,128)(2,1)S(1)}, u32[]{:S(2)}, u32[]{:S(2)}) async-start(bf16[8,8,32,128]{3,2,1,0:T(8,128)(2,1)} %broadcast_in_dim.20), calls=%async_computation.1 | async-start | bytes 1048576 | tf_op jit(solution)/shard_map/all_to_all | solution.py:31
  24.9 3.5 %turn.1.kt_hbm = bf16[8,128,2048]{2,1,0:T(8,128)(2,1)} custom-call(bf16[8,2048,128]{2,1,0:T(8,128)(2,1)} %bitcast.33), custom_call_target="tpu_custom_call" | custom-call | tf_op jit(solution)/shard_map/turn/pallas_call | solution.py:79
  28.5 6.2 %all-to-all-done.1.q_ref = bf16[8,8,32,128]{3,2,1,0:T(8,128)(2,1)S(1)} async-done(((bf16[8,8,32,128]{3,2,1,0:T(8,128)(2,1)}), bf16[8,8,32,128]{3,2,1,0:T(8,128)(2,1)S(1)}, u32[]{:S(2)}, u32[]{:S(2)}) %all-to-all-start.1) | async-done | bytes 524320 | tf_op jit(solution)/shard_map/all_to_all | solution.py:31
  34.7 7.1 %cache_attend.1 = bf16[8,272,128]{2,1,0:T(8,128)(2,1)S(1)} custom-call(s32[8]{0:T(128)S(1)} %copy-done.9, bf16[8,8,32,128]{3,2,1,0:T(8,128)(2,1)S(1)} %all-to-all-done.1.q_ref, bf16[8,128,2048]{2,1,0:T(8,128)(2,1)} %turn.1.kt_hbm, bf16[8,2048,128]{2,1,0:T(8,128)(2,1)} %bitcast.34, bf16[8,128]{1,0:T(8,128)(2,1)S(1)} %pad_maximum_fusion.kv_ref), custom_call_target="tpu_custom_call" | custom-call | tf_op jit(solution)/shard_map/cache_attend/pallas_call | solution.py:198
  41.8 13.6 %all_to_all.41.parts_ref = bf16[8,272,128]{2,1,0:T(8,128)(2,1)S(1)} all-to-all(bf16[8,272,128]{2,1,0:T(8,128)(2,1)S(1)} %cache_attend.1), channel_id=1, replica_groups=mesh['x'=4,'zh'=2,'z1'=2,'z0'=2,'yh'=2,'yl'=2,'c'=2] {'x','yh'}, dimensions={0} | all-to-all | bytes 1114112 | tf_op jit(solution)/shard_map/all_to_all | solution.py:31
  56.1 18.6 %all_to_all.42.parts_ref = bf16[8,272,128]{2,1,0:T(8,128)(2,1)S(1)} all-to-all(bf16[8,272,128]{2,1,0:T(8,128)(2,1)S(1)} %broadcast_in_dim.21), channel_id=1, replica_groups=mesh['x'=4,'zh'=2,'z1'=2,'z0'=2,'yh'=2,'yl'=2,'c'=2] {'zh','z1','z0'}, dimensions={0} | all-to-all | bytes 1114112 | tf_op jit(solution)/shard_map/all_to_all | solution.py:31
  74.6 1.3 merge_lower.1
  76.0 12.6 %all_to_all.43.heads_ref = bf16[8,32,1024]{2,1,0:T(8,128)(2,1)S(1)} all-to-all(bf16[8,32,1024]{2,1,0:T(8,128)(2,1)S(1)} %broadcast_in_dim.22), channel_id=1, replica_groups=mesh['x'=4,'zh'=2,'z1'=2,'z0'=2,'yh'=2,'yl'=2,'c'=2] {'x','yh'}, dimensions={0} | all-to-all | bytes 1048576 | tf_op jit(solution)/shard_map/all_to_all | solution.py:31
  89.0 1.2 collective-permute-done
  90.3 1.4 collective-permute-start.1
  91.7 2.9 %collective-permute-done.1 = f32[128,128]{1,0:T(8,128)S(1)} collective-permute-done((f32[128,128]{1,0:T(8,128)S(1)}, f32[128,128]{1,0:T(8,128)S(1)}, u32[]{:S(2)}, u32[]{:S(2)}) %collective-permute-start.1) | collective-permute-done | bytes 65568 | tf_op jit(solution)/shard_map/ppermute | solution.py:541
  94.7 1.2 project.1
  95.9 3.5 %all-to-all-start.5 = ((bf16[8,352,128]{2,1,0:T(8,128)(2,1)}), bf16[8,352,128]{2,1,0:T(8,128)(2,1)S(1)}, u32[]{:S(2)}, u32[]{:S(2)}) async-start(bf16[8,352,128]{2,1,0:T(8,128)(2,1)} %get-tuple-element.12), calls=%async_computation.5 | async-start | bytes 1441792 | tf_op jit(solution)/shard_map/all_to_all | solution.py:31
  99.5 1.0 split_heads.1
  100.4 3.5 %collective-permute-start.2 = (bf16[1040,128]{1,0:T(8,128)(2,1)S(1)}, bf16[1040,128]{1,0:T(8,128)(2,1)S(1)}, u32[]{:S(2)}, u32[]{:S(2)}) collective-permute-start(bf16[1040,128]{1,0:T(8,128)(2,1)S(1)} %get-tuple-element.14), channel_id=1, source_target_pairs={{0,4},{4,0},{1,5},{5,1},{2,6},{6,2},{3,7},{7,3},{8,12},{12,8},{9,1... | collective-permute-start | bytes 798728 | tf_op jit(solution)/shard_map/ppermute | solution.py:541
  104.5 1.0 collective-permute-start.4
  105.5 12.5 %all-to-all-done.5 = bf16[8,352,128]{2,1,0:T(8,128)(2,1)S(1)} async-done(((bf16[8,352,128]{2,1,0:T(8,128)(2,1)}), bf16[8,352,128]{2,1,0:T(8,128)(2,1)S(1)}, u32[]{:S(2)}, u32[]{:S(2)}) %all-to-all-start.5) | async-done | bytes 720928 | tf_op jit(solution)/shard_map/all_to_all | solution.py:31
  118.1 3.7 %collective-permute-done.2.b_ref = bf16[1040,128]{1,0:T(8,128)(2,1)S(1)} collective-permute-done((bf16[1040,128]{1,0:T(8,128)(2,1)S(1)}, bf16[1040,128]{1,0:T(8,128)(2,1)S(1)}, u32[]{:S(2)}, u32[]{:S(2)}) %collective-permute-start.2) | collective-permute-done | bytes 266272 | tf_op jit(solution)/shard_map/ppermute | solution.py:541
  121.9 15.0 %all_to_all.44.terms_ref = bf16[8,176,128]{2,1,0:T(8,128)(2,1)S(1)} all-to-all(bf16[8,176,128]{2,1,0:T(8,128)(2,1)S(1)} %bitcast.35), channel_id=1, replica_groups=mesh['x'=4,'zh'=2,'z1'=2,'z0'=2,'yh'=2,'yl'=2,'c'=2] {'zh','z1','z0'}, dimensions={0} | all-to-all | bytes 720896 | tf_op jit(solution)/shard_map/all_to_all | solution.py:31
  136.8 1.0 retained_attend.1
  137.8 10.2 %all_to_all.45.parts_ref = bf16[4,32,128]{2,1,0:T(8,128)(2,1)S(1)} all-to-all(bf16[4,32,128]{2,1,0:T(8,128)(2,1)S(1)} %retained_attend.1), channel_id=1, replica_groups=mesh['x'=4,'zh'=2,'z1'=2,'z0'=2,'yh'=2,'yl'=2,'c'=2] {'z1','yh'}, dimensions={0} | all-to-all | bytes 65536 | tf_op jit(solution)/shard_map/all_to_all | solution.py:31
  148.0 0.8 finish_upper.1
  (42 shorter events, 2.6 us)
Async XLA Ops:
  18.9 15.8 %all-to-all-start.1 = ((bf16[8,8,32,128]{3,2,1,0:T(8,128)(2,1)}), bf16[8,8,32,128]{3,2,1,0:T(8,128)(2,1)S(1)}, u32[]{:S(2)}, u32[]{:S(2)}) async-start(bf16[8,8,32,128]{3,2,1,0:T(8,128)(2,1)} %broadcast_in_dim.20), calls=%async_computation.1 | async-start | bytes 1048576 | tf_op jit(solution)/shard_map/all_to_all | solution.py:31
  24.9 3.6 %copy-start.11 = (bf16[2,256]{1,0:T(2,128)(2,1)S(1)}, bf16[2,256]{1,0:T(2,128)(2,1)}, u32[]{:S(2)}) copy-start(bf16[2,256]{1,0:T(2,128)(2,1)} %param.19) | copy-start | bytes 3076
  24.9 3.6 %copy-start.12 = (bf16[2,256]{1,0:T(2,128)(2,1)S(1)}, bf16[2,256]{1,0:T(2,128)(2,1)}, u32[]{:S(2)}) copy-start(bf16[2,256]{1,0:T(2,128)(2,1)} %param.18) | copy-start | bytes 3076
  24.9 9.7 %copy-start.9 = (s32[8]{0:T(128)S(1)}, s32[8]{0:T(128)}, u32[]{:S(2)}) copy-start(s32[8]{0:T(128)} %len_ref.3) | copy-start | bytes 100
  34.7 40.0 %copy-start.2 = (s32[8,16,16]{2,1,0:T(8,128)S(1)}, s32[8,16,16]{2,1,0:T(8,128)}, u32[]{:S(2)}) copy-start(s32[8,16,16]{2,1,0:T(8,128)} %anc_ref.3) | copy-start | bytes 24580
  41.8 46.9 %copy-start.1 = (bf16[2048,128]{1,0:T(8,128)(2,1)S(1)}, bf16[2048,128]{1,0:T(8,128)(2,1)}, u32[]{:S(2)}) copy-start(bf16[2048,128]{1,0:T(8,128)(2,1)} %weight_ref.1) | copy-start | bytes 1572868
  41.8 52.9 %copy-start = (bf16[128,2048]{1,0:T(8,128)(2,1)S(1)}, bf16[128,2048]{1,0:T(8,128)(2,1)}, u32[]{:S(2)}) copy-start(bf16[128,2048]{1,0:T(8,128)(2,1)} %wq_ref.1) | copy-start | bytes 1572868
  41.8 52.9 %copy-start.5 = (bf16[128,256]{1,0:T(8,128)(2,1)S(1)}, bf16[128,256]{1,0:T(8,128)(2,1)}, u32[]{:S(2)}) copy-start(bf16[128,256]{1,0:T(8,128)(2,1)} %wk_ref.1) | copy-start | bytes 196612
  41.8 52.9 %copy-start.6 = (bf16[128,256]{1,0:T(8,128)(2,1)S(1)}, bf16[128,256]{1,0:T(8,128)(2,1)}, u32[]{:S(2)}) copy-start(bf16[128,256]{1,0:T(8,128)(2,1)} %wv_ref.1) | copy-start | bytes 196612
  41.8 52.9 %copy-start.7 = (bf16[128,128]{1,0:T(8,128)(2,1)S(1)}, bf16[128,128]{1,0:T(8,128)(2,1)}, u32[]{:S(2)}) copy-start(bf16[128,128]{1,0:T(8,128)(2,1)} %hidden_ref.1) | copy-start | bytes 98308
  41.8 52.9 %copy-start.10 = (f32[128]{0:T(128)S(1)}, f32[128]{0:T(128)}, u32[]{:S(2)}) copy-start(f32[128]{0:T(128)} %param.25) | copy-start | bytes 1540
  56.0 43.5 %copy-start.3 = (bf16[1,512,2,128]{3,2,1,0:T(2,128)(2,1)S(1)}, bf16[1,512,2,128]{3,2,1,0:T(2,128)(2,1)}, u32[]{:S(2)}) copy-start(bf16[1,512,2,128]{3,2,1,0:T(2,128)(2,1)} %param.29) | copy-start | bytes 786436
  56.0 43.5 %copy-start.4 = (bf16[1,512,2,128]{3,2,1,0:T(2,128)(2,1)S(1)}, bf16[1,512,2,128]{3,2,1,0:T(2,128)(2,1)}, u32[]{:S(2)}) copy-start(bf16[1,512,2,128]{3,2,1,0:T(2,128)(2,1)} %param.30) | copy-start | bytes 786436
  56.0 43.5 %copy-start.8 = (s32[1,512,2]{1,2,0:T(2,128)S(1)}, s32[1,512,2]{1,2,0:T(2,128)}, u32[]{:S(2)}) copy-start(s32[1,512,2]{1,2,0:T(2,128)} %param.31) | copy-start | bytes 12292
  88.9 1.3 collective-permute-start
  90.3 4.4 %collective-permute-start.1 = (f32[128,128]{1,0:T(8,128)S(1)}, f32[128,128]{1,0:T(8,128)S(1)}, u32[]{:S(2)}, u32[]{:S(2)}) collective-permute-start(f32[128,128]{1,0:T(8,128)S(1)} %add.6), channel_id=1, source_target_pairs={{0,2},{2,0},{1,3},{3,1},{4,6},{6,4},{5,7},{7,5},{8,10},{10,8},{9,1... | collective-permute-start | bytes 196616 | tf_op jit(solution)/shard_map/ppermute | solution.py:541
  95.9 22.1 %all-to-all-start.5 = ((bf16[8,352,128]{2,1,0:T(8,128)(2,1)}), bf16[8,352,128]{2,1,0:T(8,128)(2,1)S(1)}, u32[]{:S(2)}, u32[]{:S(2)}) async-start(bf16[8,352,128]{2,1,0:T(8,128)(2,1)} %get-tuple-element.12), calls=%async_computation.5 | async-start | bytes 1441792 | tf_op jit(solution)/shard_map/all_to_all | solution.py:31
  100.4 21.4 %collective-permute-start.2 = (bf16[1040,128]{1,0:T(8,128)(2,1)S(1)}, bf16[1040,128]{1,0:T(8,128)(2,1)S(1)}, u32[]{:S(2)}, u32[]{:S(2)}) collective-permute-start(bf16[1040,128]{1,0:T(8,128)(2,1)S(1)} %get-tuple-element.14), channel_id=1, source_target_pairs={{0,4},{4,0},{1,5},{5,1},{2,6},{6,2},{3,7},{7,3},{8,12},{12,8},{9,1... | collective-permute-start | bytes 798728 | tf_op jit(solution)/shard_map/ppermute | solution.py:541
  103.9 17.9 %collective-permute-start.3 = (bf16[1040,128]{1,0:T(8,128)(2,1)S(1)}, bf16[1040,128]{1,0:T(8,128)(2,1)S(1)}, u32[]{:S(2)}, u32[]{:S(2)}) collective-permute-start(bf16[1040,128]{1,0:T(8,128)(2,1)S(1)} %get-tuple-element.16.a_ref), channel_id=1, source_target_pairs={{0,8},{8,0},{1,9},{9,1},{2,10},{10,2},{3,11},{11,3},{4,12},{12,4},... | collective-permute-start | bytes 798728 | tf_op jit(solution)/shard_map/ppermute | solution.py:541
  104.5 17.3 %collective-permute-start.4 = (bf16[1040,128]{1,0:T(8,128)(2,1)S(1)}, bf16[1040,128]{1,0:T(8,128)(2,1)S(1)}, u32[]{:S(2)}, u32[]{:S(2)}) collective-permute-start(bf16[1040,128]{1,0:T(8,128)(2,1)S(1)} %get-tuple-element.14), channel_id=1, source_target_pairs={{0,12},{4,8},{8,4},{12,0},{1,13},{5,9},{9,5},{13,1},{2,14},{6,10},... | collective-permute-start | bytes 798728 | tf_op jit(solution)/shard_map/ppermute | solution.py:541

commit v5 on v3

--- a/solution.py
+++ b/solution.py
@@ -31,8 +31,10 @@
     return lax.all_to_all(blocks, axis, split_axis=0, concat_axis=0, tiled=True)
 
 
-def spread(array, axis):
+def spread(array, axis, near=False):
     copies = jnp.broadcast_to(array, (lax.axis_size(axis), *array.shape))
+    if near:
+        copies = pltpu.with_memory_space_constraint(copies, pltpu.VMEM)
     return exchanged(copies, axis)
 
 
@@ -277,7 +279,7 @@
 
 def merge_kernel(parts_ref, q_ref, anc_ref, out_ref, scr):
     x = lax.axis_index("x")
-    head = lax.axis_index("yh")
+    own_rows = pl.ds(pl.multiple_of(16 * lax.axis_index("yh"), 16), 16)
     stats, highest, blends, sums = folded_parts(parts_ref)
     padding = jnp.zeros((HD - 4, HD), F32)
     turned = jnp.concatenate([highest[0:1], sums[0], highest[2:3], sums[1], padding], axis=0).T
@@ -295,15 +297,11 @@
         values = pltpu.roll(tree, 62, 0).astype(BF16)
         queries = jnp.concatenate(
             [
-                jnp.where(
-                    head == 0,
-                    q_ref[2 * x + j % 2, 4 * r + j // 2, 0:16, :].astype(F32),
-                    q_ref[2 * x + j % 2, 4 * r + j // 2, 16:32, :].astype(F32),
-                )
+                q_ref[2 * x + j % 2, 4 * r + j // 2, own_rows, :]
                 for j in range(GROUP)
             ],
             axis=0,
-        ).astype(BF16)
+        )
         ancestry = anc_ref[2 * x + r].astype(F32).astype(BF16)
         seen = contract(ancestry, pick.astype(BF16), ((1,), (0,))).astype(BF16)
         seen = contract(place.astype(BF16), seen, ((1,), (0,)))
@@ -361,19 +359,27 @@
     res_ref[...] = residual
     square = jnp.sum(residual * residual, axis=1, keepdims=True)
     coarse = square.astype(BF16).astype(F32)
-    lane = lax.broadcasted_iota(jnp.int32, residual.shape, 1)
-    squares = jnp.where(lane < 64, coarse, square - coarse).astype(BF16)
+    fine = square - coarse
+    lane = lax.broadcasted_iota(jnp.int32, (8, HD), 1)
     scaled = (residual * gain_ref[...]).astype(BF16)
     q = contract(scaled, wq_ref[...], ((1,), (0,))).astype(BF16)
     k = contract(scaled, wk_ref[...], ((1,), (0,))).astype(BF16)
     v = contract(scaled, wv_ref[...], ((1,), (0,))).astype(BF16)
     for h in range(2):
         blocks = [q[:, (8 * h + g) * HD : (8 * h + g + 1) * HD] for g in range(8)]
-        blocks += [k[:, h * HD : (h + 1) * HD], v[:, h * HD : (h + 1) * HD], squares]
+        blocks += [k[:, h * HD : (h + 1) * HD], v[:, h * HD : (h + 1) * HD]]
         for r in range(8):
+            at = (r % 2) * 168
+            dest = 2 * (r // 2) + h
             for b, block in enumerate(blocks):
-                at = (r % 2) * 176 + 16 * b
-                out_ref[2 * (r // 2) + h, at : at + 16, :] = block[16 * r : 16 * r + 16]
+                out_ref[dest, at + 16 * b : at + 16 * b + 16, :] = block[16 * r : 16 * r + 16]
+            low, high = slice(16 * r, 16 * r + 8), slice(16 * r + 8, 16 * r + 16)
+            squares = jnp.where(
+                lane < 64,
+                jnp.where(lane < 32, coarse[low], fine[low]),
+                jnp.where(lane < 96, coarse[high], fine[high]),
+            )
+            out_ref[dest, at + 160 : at + 168, :] = squares.astype(BF16)
 
 
 def project(hidden, terms, gain, wq, wk, wv):
@@ -382,7 +388,7 @@
         project_kernel,
         out_shape=(
             jax.ShapeDtypeStruct((rows, HD), F32),
-            jax.ShapeDtypeStruct((GROUP, 352, HD), BF16),
+            jax.ShapeDtypeStruct((GROUP, 336, HD), BF16),
         ),
         compiler_params=pltpu.CompilerParams(vmem_limit_bytes=8 << 20),
         name="project",
@@ -425,11 +431,16 @@
     )(lengths, keys, values, positions)
 
 
-def retained_kernel(width, sum_ref, mine_ref, other_ref, anc_ref, out_ref, blend_scr, stat_scr):
+def retained_kernel(width, terms_ref, mine_ref, other_ref, anc_ref, out_ref, blend_scr, stat_scr):
     request = lax.axis_index(SEQ) // GROUP
     leader = lax.axis_index("zl") == 0
-    raw = sum_ref[...].astype(F32)
-    square = raw[160:176, 0:1] + raw[160:176, 64:65]
+    raw = terms_ref[0].astype(F32)
+    for z in range(1, GROUP):
+        raw = raw + terms_ref[z].astype(F32)
+    tile = raw[160:168]
+    square = jnp.concatenate(
+        [tile[:, 0:1] + tile[:, 32:33], tile[:, 64:65] + tile[:, 96:97]], axis=0
+    )
     inverse = lax.rsqrt(square / width + EPS)
 
     def up(b):
@@ -486,7 +497,7 @@
         out_ref[j, 16:32, :] = stat_scr[16 * j : 16 * j + 16, :].astype(BF16)
 
 
-def retained_attend(width, summed, mine, other, ancestors):
+def retained_attend(width, terms, mine, other, ancestors):
     vmem = pl.BlockSpec(memory_space=pltpu.VMEM)
     return pl.pallas_call(
         functools.partial(retained_kernel, width),
@@ -496,7 +507,7 @@
         scratch_shapes=[pltpu.VMEM((HD, HD), F32), pltpu.VMEM((HD, HD), F32)],
         compiler_params=pltpu.CompilerParams(vmem_limit_bytes=8 << 20),
         name="retained_attend",
-    )(summed, mine, other, ancestors)
+    )(terms, mine, other, ancestors)
 
 
 def finish_kernel(parts_ref, out_ref):
@@ -570,7 +581,7 @@
         retained_index[0].T,
     )
     kept_other = swapped(kept_given, "yh")
-    queries = spread(spread(own_q, DEPTH).reshape(-1, HD), FACE).reshape(GROUP, GROUP, 32, HD)
+    queries = spread(spread(own_q, DEPTH), FACE, True)
     turned_keys = turn(cache_keys.reshape(requests, cache_part * kv_heads, HD))
     parts = cache_attend(
         cache_lengths,
@@ -588,10 +599,10 @@
         tree_hidden, terms, norm_gain.reshape(1, -1), w_query_up, w_key_up, w_value_up
     )
     summed = jnp.sum(exchanged(projected, FACE).astype(F32), axis=0).astype(BF16)
-    shares = jnp.broadcast_to(summed.reshape(2, 1, 176, HD), (2, 4, 176, HD))
-    arrived = exchanged(shares.reshape(GROUP, 176, HD), DEPTH)
-    mine = jnp.sum(arrived.astype(F32), axis=0).astype(BF16)
-    upper = retained_attend(width, mine, kept_own, kept_other, ancestors)
+    shares = jnp.broadcast_to(summed.reshape(2, 1, 168, HD), (2, 4, 168, HD))
+    shares = pltpu.with_memory_space_constraint(shares.reshape(GROUP, 168, HD), pltpu.VMEM)
+    arrived = exchanged(shares, DEPTH)
+    upper = retained_attend(width, arrived, kept_own, kept_other, ancestors)
     upper_heads = finish_upper(exchanged(upper, TEAM))
     return (residual, upper_heads)
 

time: 140 us -> 140 us (level)
    all_to_all x2, waiting for transfers between devices: 15.5 us -> 8.51 us  [exchanged(): return lax.all_to_all(blocks, axis, split_axis=0, concat_axis=0, tiled=True)]
    ppermute x3, waiting for transfers between devices: 4.16 us -> 11 us  [swapped(): return lax.ppermute(array, axis, [(0, 1), (1, 0)])]
  transfers between devices with their start and end apart: 5 -> 5, of which waited for: 4 -> 5; matrix products, arithmetic and copies ran while one was open for 0% -> 0% of each run, Pallas kernels for 3% -> 3%
where the time goes in v5:
time: 140 us; the launch traced here: 139 us
  blocking collectives  87.9 us (63%)
  waiting for transfers between devices  19.5 us (14%)
  Pallas kernels  15.9 us (11%)
  starting transfers between devices  12.2 us (9%)
  local copies, waits for them, and re-layouts  2.58 us (2%)
    all_to_all x6, blocking collectives, exchanged(): return lax.all_to_all(blocks, axis, split_axis=0, concat_axis=0, tiled=True)  87.9 us
    ppermute x3, waiting for transfers between devices, swapped(): return lax.ppermute(array, axis, [(0, 1), (1, 0)])  11 us
    all_to_all x2, starting transfers between devices, exchanged(): return lax.all_to_all(blocks, axis, split_axis=0, concat_axis=0, tiled=True)  9.47 us
    all_to_all x2, waiting for transfers between devices, exchanged(): return lax.all_to_all(blocks, axis, split_axis=0, concat_axis=0, tiled=True)  8.51 us
    pallas_call x1, Pallas kernels, cache_attend(): pl.pallas_call(cache_kernel, in_specs=[pl.BlockSpec(memory_space=pltpu.SM...  7.08 us
    pallas_call x1, Pallas kernels, turn(): pl.pallas_call(turn_kernel, in_specs=[pl.BlockSpec(memory_space=pltpu.HBM...  3.53 us
  transfers between devices with their start and end apart: 5, of which 5 were waited for; matrix products, arithmetic and copies ran while one was open for 0% of the time, Pallas kernels for 3%

profile of v5, /device:TPU:8, one launch (start us, length us, event | category | flops | bytes accessed | tf_op | source)
XLA Modules:
  0.0 139.0 jit_solution(17195727616608986851)
XLA Ops:
  0.6 0.7 copy.27
  1.4 16.6 %all_to_all.40 = bf16[8,32,128]{2,1,0:T(8,128)(2,1)S(1)} all-to-all(bf16[8,32,128]{2,1,0:T(8,128)(2,1)S(1)} %broadcast_in_dim.19), channel_id=1, replica_groups=mesh['x'=4,'zh'=2,'zl'=4,'yh'=2,'yl'=2,'c'=2] {'zh','zl'}, dimensions={0} | all-to-all | bytes 131072 | tf_op jit(solution)/shard_map/all_to_all | solution.py:31
  18.0 0.9 broadcast_in_dim.20
  18.9 6.0 %all-to-all-start.1 = ((bf16[8,8,32,128]{3,2,1,0:T(8,128)(2,1)}), bf16[8,8,32,128]{3,2,1,0:T(8,128)(2,1)S(1)}, u32[]{:S(2)}, u32[]{:S(2)}) async-start(bf16[8,8,32,128]{3,2,1,0:T(8,128)(2,1)} %broadcast_in_dim.20), calls=%async_computation.1 | async-start | bytes 1048576 | tf_op jit(solution)/shard_map/all_to_all | solution.py:31
  24.9 3.5 %turn.1.kt_hbm = bf16[8,128,2048]{2,1,0:T(8,128)(2,1)} custom-call(bf16[8,2048,128]{2,1,0:T(8,128)(2,1)} %bitcast.33), custom_call_target="tpu_custom_call" | custom-call | tf_op jit(solution)/shard_map/turn/pallas_call | solution.py:79
  28.5 6.2 %all-to-all-done.1.q_ref = bf16[8,8,32,128]{3,2,1,0:T(8,128)(2,1)S(1)} async-done(((bf16[8,8,32,128]{3,2,1,0:T(8,128)(2,1)}), bf16[8,8,32,128]{3,2,1,0:T(8,128)(2,1)S(1)}, u32[]{:S(2)}, u32[]{:S(2)}) %all-to-all-start.1) | async-done | bytes 524320 | tf_op jit(solution)/shard_map/all_to_all | solution.py:31
  34.7 7.1 %cache_attend.1 = bf16[8,272,128]{2,1,0:T(8,128)(2,1)S(1)} custom-call(s32[8]{0:T(128)S(1)} %copy-done.9, bf16[8,8,32,128]{3,2,1,0:T(8,128)(2,1)S(1)} %all-to-all-done.1.q_ref, bf16[8,128,2048]{2,1,0:T(8,128)(2,1)} %turn.1.kt_hbm, bf16[8,2048,128]{2,1,0:T(8,128)(2,1)} %bitcast.34, bf16[8,128]{1,0:T(8,128)(2,1)S(1)} %pad_maximum_fusion.kv_ref), custom_call_target="tpu_custom_call" | custom-call | tf_op jit(solution)/shard_map/cache_attend/pallas_call | solution.py:198
  41.8 13.6 %all_to_all.41.parts_ref = bf16[8,272,128]{2,1,0:T(8,128)(2,1)S(1)} all-to-all(bf16[8,272,128]{2,1,0:T(8,128)(2,1)S(1)} %cache_attend.1), channel_id=1, replica_groups=mesh['x'=4,'zh'=2,'zl'=4,'yh'=2,'yl'=2,'c'=2] {'x','yh'}, dimensions={0} | all-to-all | bytes 1114112 | tf_op jit(solution)/shard_map/all_to_all | solution.py:31
  56.1 18.4 %all_to_all.42.parts_ref = bf16[8,272,128]{2,1,0:T(8,128)(2,1)S(1)} all-to-all(bf16[8,272,128]{2,1,0:T(8,128)(2,1)S(1)} %broadcast_in_dim.21), channel_id=1, replica_groups=mesh['x'=4,'zh'=2,'zl'=4,'yh'=2,'yl'=2,'c'=2] {'zh','zl'}, dimensions={0} | all-to-all | bytes 1114112 | tf_op jit(solution)/shard_map/all_to_all | solution.py:31
  74.5 1.3 merge_lower.1
  75.8 12.6 %all_to_all.43.heads_ref = bf16[8,32,1024]{2,1,0:T(8,128)(2,1)S(1)} all-to-all(bf16[8,32,1024]{2,1,0:T(8,128)(2,1)S(1)} %broadcast_in_dim.22), channel_id=1, replica_groups=mesh['x'=4,'zh'=2,'zl'=4,'yh'=2,'yl'=2,'c'=2] {'x','yh'}, dimensions={0} | all-to-all | bytes 1048576 | tf_op jit(solution)/shard_map/all_to_all | solution.py:31
  88.8 1.2 collective-permute-done
  90.1 1.4 %collective-permute-start.1 = (f32[128,128]{1,0:T(8,128)S(1)}, f32[128,128]{1,0:T(8,128)S(1)}, u32[]{:S(2)}, u32[]{:S(2)}) collective-permute-start(f32[128,128]{1,0:T(8,128)S(1)} %add.6), channel_id=1, source_target_pairs={{0,2},{2,0},{1,3},{3,1},{4,6},{6,4},{5,7},{7,5},{8,10},{10,8},{9,1... | collective-permute-start | bytes 196616 | tf_op jit(solution)/shard_map/ppermute | solution.py:544
  91.5 2.9 %collective-permute-done.1 = f32[128,128]{1,0:T(8,128)S(1)} collective-permute-done((f32[128,128]{1,0:T(8,128)S(1)}, f32[128,128]{1,0:T(8,128)S(1)}, u32[]{:S(2)}, u32[]{:S(2)}) %collective-permute-start.1) | collective-permute-done | bytes 65568 | tf_op jit(solution)/shard_map/ppermute | solution.py:544
  95.2 15.2 %all_to_all.44 = bf16[8,336,128]{2,1,0:T(8,128)(2,1)S(1)} all-to-all(bf16[8,336,128]{2,1,0:T(8,128)(2,1)S(1)} %get-tuple-element.7), channel_id=1, replica_groups=mesh['x'=4,'zh'=2,'zl'=4,'yh'=2,'yl'=2,'c'=2] {'x','yh'}, dimensions={0} | all-to-all | bytes 1376256 | tf_op jit(solution)/shard_map/all_to_all | solution.py:31
  110.5 0.8 broadcast_in_dim.24
  111.3 3.4 %all-to-all-start.6 = ((bf16[8,168,128]{2,1,0:T(8,128)(2,1)}), bf16[8,168,128]{2,1,0:T(8,128)(2,1)S(1)}, u32[]{:S(2)}, u32[]{:S(2)}) async-start(bf16[8,168,128]{2,1,0:T(8,128)(2,1)} %bitcast.12), calls=%async_computation.6 | async-start | bytes 688128 | tf_op jit(solution)/shard_map/all_to_all | solution.py:31
  114.7 1.0 split_heads.1
  115.7 1.2 collective-permute-start.2
  116.9 6.8 %collective-permute-done.2.other_ref = bf16[1040,128]{1,0:T(8,128)(2,1)S(1)} collective-permute-done((bf16[1040,128]{1,0:T(8,128)(2,1)S(1)}, bf16[1040,128]{1,0:T(8,128)(2,1)S(1)}, u32[]{:S(2)}, u32[]{:S(2)}) %collective-permute-start.2) | collective-permute-done | bytes 266272 | tf_op jit(solution)/shard_map/ppermute | solution.py:544
  123.7 2.4 %all-to-all-done.6.terms_ref = bf16[8,168,128]{2,1,0:T(8,128)(2,1)S(1)} async-done(((bf16[8,168,128]{2,1,0:T(8,128)(2,1)}), bf16[8,168,128]{2,1,0:T(8,128)(2,1)S(1)}, u32[]{:S(2)}, u32[]{:S(2)}) %all-to-all-start.6) | async-done | bytes 344096 | tf_op jit(solution)/shard_map/all_to_all | solution.py:31
  126.1 0.8 retained_attend.1
  126.8 11.4 %all_to_all.45.parts_ref = bf16[8,32,128]{2,1,0:T(8,128)(2,1)S(1)} all-to-all(bf16[8,32,128]{2,1,0:T(8,128)(2,1)S(1)} %retained_attend.1), channel_id=1, replica_groups=mesh['x'=4,'zh'=2,'zl'=4,'yh'=2,'yl'=2,'c'=2] {'zl','yh'}, dimensions={0} | all-to-all | bytes 131072 | tf_op jit(solution)/shard_map/all_to_all | solution.py:31
  138.2 0.8 finish_upper.1
  (38 shorter events, 1.9 us)
Async XLA Ops:
  18.9 15.8 %all-to-all-start.1 = ((bf16[8,8,32,128]{3,2,1,0:T(8,128)(2,1)}), bf16[8,8,32,128]{3,2,1,0:T(8,128)(2,1)S(1)}, u32[]{:S(2)}, u32[]{:S(2)}) async-start(bf16[8,8,32,128]{3,2,1,0:T(8,128)(2,1)} %broadcast_in_dim.20), calls=%async_computation.1 | async-start | bytes 1048576 | tf_op jit(solution)/shard_map/all_to_all | solution.py:31
  24.9 3.6 %copy-start.11 = (bf16[2,256]{1,0:T(2,128)(2,1)S(1)}, bf16[2,256]{1,0:T(2,128)(2,1)}, u32[]{:S(2)}) copy-start(bf16[2,256]{1,0:T(2,128)(2,1)} %param.19) | copy-start | bytes 3076
  24.9 3.6 %copy-start.12 = (bf16[2,256]{1,0:T(2,128)(2,1)S(1)}, bf16[2,256]{1,0:T(2,128)(2,1)}, u32[]{:S(2)}) copy-start(bf16[2,256]{1,0:T(2,128)(2,1)} %param.18) | copy-start | bytes 3076
  24.9 9.7 %copy-start.9 = (s32[8]{0:T(128)S(1)}, s32[8]{0:T(128)}, u32[]{:S(2)}) copy-start(s32[8]{0:T(128)} %len_ref.3) | copy-start | bytes 100
  34.7 39.8 %copy-start.4 = (s32[8,16,16]{2,1,0:T(8,128)S(1)}, s32[8,16,16]{2,1,0:T(8,128)}, u32[]{:S(2)}) copy-start(s32[8,16,16]{2,1,0:T(8,128)} %anc_ref.3) | copy-start | bytes 24580
  41.8 46.7 %copy-start.1 = (bf16[2048,128]{1,0:T(8,128)(2,1)S(1)}, bf16[2048,128]{1,0:T(8,128)(2,1)}, u32[]{:S(2)}) copy-start(bf16[2048,128]{1,0:T(8,128)(2,1)} %weight_ref.1) | copy-start | bytes 1572868
  41.8 52.7 %copy-start = (bf16[128,2048]{1,0:T(8,128)(2,1)S(1)}, bf16[128,2048]{1,0:T(8,128)(2,1)}, u32[]{:S(2)}) copy-start(bf16[128,2048]{1,0:T(8,128)(2,1)} %wq_ref.1) | copy-start | bytes 1572868
  41.8 52.7 %copy-start.5 = (bf16[128,256]{1,0:T(8,128)(2,1)S(1)}, bf16[128,256]{1,0:T(8,128)(2,1)}, u32[]{:S(2)}) copy-start(bf16[128,256]{1,0:T(8,128)(2,1)} %wk_ref.1) | copy-start | bytes 196612
  41.8 52.7 %copy-start.6 = (bf16[128,256]{1,0:T(8,128)(2,1)S(1)}, bf16[128,256]{1,0:T(8,128)(2,1)}, u32[]{:S(2)}) copy-start(bf16[128,256]{1,0:T(8,128)(2,1)} %wv_ref.1) | copy-start | bytes 196612
  41.8 52.7 %copy-start.7 = (bf16[128,128]{1,0:T(8,128)(2,1)S(1)}, bf16[128,128]{1,0:T(8,128)(2,1)}, u32[]{:S(2)}) copy-start(bf16[128,128]{1,0:T(8,128)(2,1)} %hidden_ref.1) | copy-start | bytes 98308
  41.8 52.7 %copy-start.10 = (f32[128]{0:T(128)S(1)}, f32[128]{0:T(128)}, u32[]{:S(2)}) copy-start(f32[128]{0:T(128)} %param.25) | copy-start | bytes 1540
  74.5 40.2 %copy-start.2 = (bf16[1,512,2,128]{3,2,1,0:T(2,128)(2,1)S(1)}, bf16[1,512,2,128]{3,2,1,0:T(2,128)(2,1)}, u32[]{:S(2)}) copy-start(bf16[1,512,2,128]{3,2,1,0:T(2,128)(2,1)} %param.29) | copy-start | bytes 786436
  74.5 40.2 %copy-start.3 = (bf16[1,512,2,128]{3,2,1,0:T(2,128)(2,1)S(1)}, bf16[1,512,2,128]{3,2,1,0:T(2,128)(2,1)}, u32[]{:S(2)}) copy-start(bf16[1,512,2,128]{3,2,1,0:T(2,128)(2,1)} %param.30) | copy-start | bytes 786436
  74.5 40.2 %copy-start.8 = (s32[1,512,2]{1,2,0:T(2,128)S(1)}, s32[1,512,2]{1,2,0:T(2,128)}, u32[]{:S(2)}) copy-start(s32[1,512,2]{1,2,0:T(2,128)} %param.31) | copy-start | bytes 12292
  88.7 1.3 collective-permute-start
  90.1 4.4 %collective-permute-start.1 = (f32[128,128]{1,0:T(8,128)S(1)}, f32[128,128]{1,0:T(8,128)S(1)}, u32[]{:S(2)}, u32[]{:S(2)}) collective-permute-start(f32[128,128]{1,0:T(8,128)S(1)} %add.6), channel_id=1, source_target_pairs={{0,2},{2,0},{1,3},{3,1},{4,6},{6,4},{5,7},{7,5},{8,10},{10,8},{9,1... | collective-permute-start | bytes 196616 | tf_op jit(solution)/shard_map/ppermute | solution.py:544
  111.3 14.8 %all-to-all-start.6 = ((bf16[8,168,128]{2,1,0:T(8,128)(2,1)}), bf16[8,168,128]{2,1,0:T(8,128)(2,1)S(1)}, u32[]{:S(2)}, u32[]{:S(2)}) async-start(bf16[8,168,128]{2,1,0:T(8,128)(2,1)} %bitcast.12), calls=%async_computation.6 | async-start | bytes 688128 | tf_op jit(solution)/shard_map/all_to_all | solution.py:31
  115.7 8.0 %collective-permute-start.2 = (bf16[1040,128]{1,0:T(8,128)(2,1)S(1)}, bf16[1040,128]{1,0:T(8,128)(2,1)S(1)}, u32[]{:S(2)}, u32[]{:S(2)}) collective-permute-start(bf16[1040,128]{1,0:T(8,128)(2,1)S(1)} %get-tuple-element.9), channel_id=1, source_target_pairs={{0,4},{4,0},{1,5},{5,1},{2,6},{6,2},{3,7},{7,3},{8,12},{12,8},{9,1... | collective-permute-start | bytes 798728 | tf_op jit(solution)/shard_map/ppermute | solution.py:544
